TPU v7x, 32 devices: a whole 2x2x4 slice. The times are simulated.
32 devices in a mesh: chan: 16 (over z, y, core), tm: 2 (over x).
Axes of the slice: x: 2, y: 2, z: 4, core: 2. Of those that a mesh axis runs over, the one named last changes fastest.
Arguments:
- traces: float32 [8, 1024, 1500], P('tm', 'chan'), may hold values from -6 to 6
- plan: int32 [16, 3], P('chan'), may hold values 0 or 1
- dead_channels: int32 [96], replicated, may hold values from 0 to 1023
Outputs:
- correlations: float32 [16, 64, 3, 64, 129], P('chan', 'tm')
Inputs may be any that keep to these rules, and one draw needn't show every extreme that they name: `dead_channels`: entries may repeat.
All inputs are finite; a program needn't handle non-finite values. No bound on the sum of `plan` on one device may be relied on, other than what follows from the above.
Results may differ from a plain program's by a relative error of at most 0.0085.
Values may be sent and summed in bfloat16 or wider, within the bound.
No kernel may reach another device: no remote copies, remote signals or barrier semaphores. Data moves between devices by JAX's collectives and lax.ppermute only.
A program may use at most 64 MiB of HBM per device.

v0:
```python
import math

import jax
import jax.numpy as jnp
from jax import lax
from jax.sharding import PartitionSpec as P

BINS = 128
HALF_LAG = 64
OFFS = 3


WATER_LEVEL = 0.1
EPSILON = 1e-06


def shifted(value, axis, steps):
    count = lax.axis_size(axis)
    pairs = [(source, (source + steps) % count) for source in range(count)]
    return lax.ppermute(value, axis, pairs)


def dft_table(samples, freq_bins):
    frequency = jnp.arange(1, freq_bins + 1, dtype=jnp.int32)
    sample_index = jnp.arange(samples, dtype=jnp.int32)
    phases = jnp.mod(sample_index[:, None] * frequency[None, :], samples).astype(jnp.float32) * (
        2.0 * math.pi / samples
    )
    return jnp.concatenate([jnp.cos(phases), -jnp.sin(phases)], axis=1)


def lag_table(samples, freq_bins, half_lag, scale):
    frequency = jnp.arange(1, freq_bins + 1, dtype=jnp.int32)
    lag_index = jnp.arange(-half_lag, half_lag + 1, dtype=jnp.int32)
    phases = jnp.mod(frequency[:, None] * lag_index[None, :], samples).astype(jnp.float32) * (
        2.0 * math.pi / samples
    )
    return jnp.concatenate([jnp.cos(phases), -jnp.sin(phases)], axis=0) * scale


def whiten(raw_traces, dft_matrix, live_mask, freq_bins):
    windows, channels, samples = raw_traces.shape
    spectra = jnp.dot(
        raw_traces.reshape(windows * channels, samples), dft_matrix, precision=lax.Precision.HIGHEST
    )
    spectra = spectra.reshape(windows, channels, 2 * freq_bins)
    real_part = spectra[..., :freq_bins]
    imag_part = spectra[..., freq_bins:]
    powers = real_part * real_part + imag_part * imag_part
    mean_power = jnp.mean(powers, axis=-1, keepdims=True)
    denominator = jnp.sqrt(powers + WATER_LEVEL * mean_power + EPSILON)
    whitened = jnp.concatenate([real_part / denominator, imag_part / denominator], axis=-1)
    return whitened * live_mask[None, :, None]


def cross_spectra(own_block, far_block, freq_bins):
    own_real = own_block[:, :, None, :freq_bins]
    own_imag = own_block[:, :, None, freq_bins:]
    far_real = far_block[:, None, :, :freq_bins]
    far_imag = far_block[:, None, :, freq_bins:]
    real_part = jnp.sum(own_real * far_real + own_imag * far_imag, axis=0)
    imag_part = jnp.sum(own_imag * far_real - own_real * far_imag, axis=0)
    return jnp.concatenate([real_part, imag_part], axis=-1)


def shards(traces, plan, dead_channels):
    windows, block_width, samples = traces.shape
    total_windows = windows * lax.axis_size("tm")
    first_channel = lax.axis_index("chan") * block_width
    chan_ids = first_channel + jnp.arange(block_width, dtype=jnp.int32)
    live_mask = 1.0 - jnp.any(dead_channels[:, None] == chan_ids[None, :], axis=0).astype(
        jnp.float32
    )
    own_spectra = whiten(traces, dft_table(samples, BINS), live_mask, BINS)
    upper_mask = (jnp.arange(block_width)[None, :] > jnp.arange(block_width)[:, None]).astype(
        jnp.float32
    )
    weights = plan[0].astype(jnp.float32)
    lag_matrix = lag_table(samples, BINS, HALF_LAG, 1.0 / math.sqrt(BINS * total_windows))
    lag_count = lag_matrix.shape[1]
    share = block_width // lax.axis_size("tm")
    pieces = [cross_spectra(own_spectra, own_spectra, BINS) * (upper_mask * weights[0])[:, :, None]]
    moving = own_spectra
    for offset in range(1, OFFS):
        moving = shifted(moving.astype(jnp.bfloat16), "chan", 1).astype(moving.dtype)
        pieces.append(cross_spectra(own_spectra, moving, BINS) * weights[offset])
    partial_value = jnp.stack(pieces, axis=1)
    lagged = jnp.dot(
        partial_value.reshape(-1, 2 * BINS), lag_matrix, precision=lax.Precision.HIGHEST
    )
    result = lax.psum_scatter(
        lagged.reshape(lax.axis_size("tm") * share, OFFS, block_width, lag_count).astype(
            jnp.bfloat16
        ),
        "tm",
        scatter_dimension=0,
        tiled=True,
    ).astype(jnp.float32)
    return result[None]


def solution(mesh):
    in_specs = (P("tm", "chan", None), P("chan", None), P())
    out_specs = P("chan", "tm", None, None, None)
    return jax.shard_map(shards, mesh=mesh, in_specs=in_specs, out_specs=out_specs, check_vma=False)
```

profile of v0, /device:TPU:0, one launch (start us, length us, event | category | flops | bytes accessed | tf_op | source)
XLA Modules:
  0.0 144.6 jit_solution(4522204812830243042)
XLA Ops:
  6.5 0.0 copy-start
  6.5 0.0 copy-start.1
  6.5 0.0 copy-start.2
  6.5 0.0 reduce-scatter.2.cloned.1.call-start
  6.6 3.1 %fusion.17 = (f32[1500,128]{1,0:T(8,128)S(1)}, f32[1500,128]{1,0:T(8,128)S(1)}) fusion(s32[128]{0:T(128)S(1)} %iota_add_fusion.2), kind=kLoop, calls=%fused_computation.28 | loop fusion | flops 1920000 | bytes 1536512 | tf_op jit(solution)/shard_map/cos | solution.py:29
  9.7 0.0 copy-done
  9.7 1.6 %fusion.9 = f32[256,256]{0,1:T(8,128)S(1)} fusion(f32[256,1500]{1,0:T(8,128)S(1)} %bitcast.22, f32[1500,128]{1,0:T(8,128)S(1)} %get-tuple-element.31, f32[1500,128]{1,0:T(8,128)S(1)} %get-tuple-element.30), kind=kOutput, calls=%fused_computation.17 | convolution fusion | flops 1180032000 | bytes 3334144 | tf_op jit(solution)/shard_map/dot_general | solution.py:43
  11.3 0.1 fusion.34
  11.4 0.1 slice_divide_fusion.1
  11.6 0.0 copy-done.1
  11.6 0.2 compare_reduce_fusion
  11.8 0.1 fusion.35
  11.9 0.5 collective-permute-start
  12.5 0.0 copy-done.2
  12.5 1.0 fusion.28
  13.5 0.6 fusion.39
  14.2 0.7 fusion.30
  14.8 5.3 %collective-permute-done = bf16[4,64,256]{2,1,0:T(8,128)(2,1)S(1)} collective-permute-done((bf16[4,64,256]{2,1,0:T(8,128)(2,1)S(1)}, bf16[4,64,256]{2,1,0:T(8,128)(2,1)S(1)}, u32[]{:S(2)}, u32[]{:S(2)}) %collective-permute-start) | collective-permute-done | bytes 131104 | tf_op jit(solution)/shard_map/ppermute | solution.py:20
  20.1 0.0 collective-permute-start.1
  20.1 7.1 %collective-permute-done.1 = bf16[4,64,256]{2,1,0:T(8,128)(2,1)S(1)} collective-permute-done((bf16[4,64,256]{2,1,0:T(8,128)(2,1)S(1)}, bf16[4,64,256]{2,1,0:T(8,128)(2,1)S(1)}, u32[]{:S(2)}, u32[]{:S(2)}) %collective-permute-start.1) | collective-permute-done | bytes 131104 | tf_op jit(solution)/shard_map/ppermute | solution.py:20
  27.2 13.6 %add_reduce_fusion.1 = (f32[64,64,128]{2,1,0:T(8,128)S(1)}, f32[64,64,128]{2,1,0:T(8,128)S(1)}, f32[64,64,128]{2,1,0:T(8,128)S(1)}, f32[64,64,128]{2,1,0:T(8,128...) fusion(f32[4,64,128]{2,1,0:T(8,128)S(1)} %get-tuple-element.24, f32[4,64,128]{2,1,0:T(8,128)S(1)} %get-tuple-element.23, ...), kind=kLoop, calls=%fused_computation.9 | loop fusion | flops 47185920 | bytes 13369344 | tf_op jit(solution)/shard_map/reduce_sum | solution.py:61
  40.8 0.7 maximum_multiply_fusion
  41.6 2.2 %maximum_multiply_fusion.1 = (f32[64,1,64,256]{3,2,1,0:T(8,128)S(1)}, f32[64,1,64,256]{3,2,1,0:T(8,128)S(1)}) fusion(f32[64,1,64,128]{3,2,1,0:T(8,128)S(1)} %bitcast.24, f32[64,1,64,128]{3,2,1,0:T(8,128)S(1)} %bitcast.23, f32[]{:T(128)} %bitcast.9, f32[]{:T(128)} %bitcast.12, f32[64,1,64,128]{3,2,1,0:T(8,128)S(1)} %bitcast.25, f32[64,1,64,128]{3,2,1,0:T(8,128)S(1)} %bitcast.26), kind=kLoop, calls=%fused_computation.13 | loop fusion | flops 4194304 | bytes 16777224 | tf_op jit(solution)/shard_map/mul | solution.py:86
  43.8 13.5 %fusion.6 = bf16[64,3,64,129]{3,2,1,0:T(8,128)(2,1)} fusion(f32[64,1,64,256]{3,2,1,0:T(8,128)S(1)} %get-tuple-element.33, f32[64,1,64,256]{3,2,1,0:T(8,128)S(1)} %get-tuple-element.32, f32[64,1,64,256]{3,2,1,0:T(8,128)S(1)} %maximum_multiply_fusion, f32[128,129]{0,1:T(8,128)} %get-tuple-element.26, f32[128,129]{0,1:T(8,128)} %get-tuple-element.25), kind=kOutput, calls=%fused_computation.15 | convolution fusion | flops 4877529600 | bytes 15885312 | tf_op jit(solution)/shard_map/dot_general | solution.py:88
  57.3 0.0 reduce-scatter.2.cloned.1.call-update
  57.3 75.0 %reduce-scatter.2.cloned.1.call-done = bf16[32,3,64,129]{3,2,1,0:T(8,128)(2,1)} async-done(((bf16[64,3,64,129]{3,2,1,0:T(8,128)(2,1)}), bf16[32,3,64,129]{3,2,1,0:T(8,128)(2,1)}) %reduce-scatter.2.cloned.1.call-update) | async-done | bytes 1585168 | tf_op jit(solution)/shard_map/reduce_scatter | solution.py:91
  132.3 5.5 %bitcast_convert_fusion = f32[1,32,3,64,129]{4,3,2,1,0:T(8,128)} fusion(bf16[32,3,64,129]{3,2,1,0:T(8,128)(2,1)} %reduce-scatter.2.cloned.1.call-done), kind=kLoop, calls=%fused_computation.16 | loop fusion | flops 792576 | bytes 4755456 | tf_op jit(solution)/shard_map/broadcast_in_dim | solution.py:99
  (9 shorter events, 0.1 us)
Async XLA Ops:
  6.5 3.2 %copy-start = (f32[4,64,1500]{2,1,0:T(8,128)S(1)}, f32[4,64,1500]{2,1,0:T(8,128)}, u32[]{:S(2)}) copy-start(f32[4,64,1500]{2,1,0:T(8,128)} %param.3) | copy-start | bytes 4608004
  6.5 5.1 %copy-start.1 = (s32[96]{0:T(128)S(1)}, s32[96]{0:T(128)}, u32[]{:S(2)}) copy-start(s32[96]{0:T(128)} %param.5) | copy-start | bytes 1156
  6.5 5.9 %copy-start.2 = (s32[1,3]{1,0:T(1,128)S(1)}, s32[1,3]{1,0:T(1,128)}, u32[]{:S(2)}) copy-start(s32[1,3]{1,0:T(1,128)} %param.4) | copy-start | bytes 40
  6.5 125.8 %reduce-scatter.2.cloned.1.call-start = ((), (), s32[]{:S(2)}) async-start(), calls=%async_computation.1 | async-start | bytes 9437184 | tf_op jit(solution)/shard_map/reduce_scatter | solution.py:91
  11.9 8.2 %collective-permute-start = (bf16[4,64,256]{2,1,0:T(8,128)(2,1)S(1)}, bf16[4,64,256]{2,1,0:T(8,128)(2,1)S(1)}, u32[]{:S(2)}, u32[]{:S(2)}) collective-permute-start(bf16[4,64,256]{2,1,0:T(8,128)(2,1)S(1)} %get-tuple-element.15), channel_id=1, source_target_pairs={{0,2},{2,4},{4,6},{6,8},{8,10},{10,12},{12,14},{14,16},{16,18},{18... | collective-permute-start | bytes 393224 | tf_op jit(solution)/shard_map/ppermute | solution.py:20
  20.1 7.1 %collective-permute-start.1 = (bf16[4,64,256]{2,1,0:T(8,128)(2,1)S(1)}, bf16[4,64,256]{2,1,0:T(8,128)(2,1)S(1)}, u32[]{:S(2)}, u32[]{:S(2)}) collective-permute-start(bf16[4,64,256]{2,1,0:T(8,128)(2,1)S(1)} %collective-permute-done), channel_id=1, source_target_pairs={{0,2},{2,4},{4,6},{6,8},{8,10},{10,12},{12,14},{14,16},{16,18},{18... | collective-permute-start | bytes 393224 | tf_op jit(solution)/shard_map/ppermute | solution.py:20
Sparse Core Ops, SparseCore 0:
  57.5 74.8 reduce-scatter.1
where the time goes:
time: 145 us
  waiting for transfers between devices  87.3 us (60%)
  other arithmetic  27.4 us (19%)
  matrix products  15.1 us (10%)
  between operations  13.5 us (9%)
    reduce_scatter x1, waiting for transfers between devices, shards(): lax.psum_scatter(lagged.reshape(lax.axis_size('tm') * share, OFFS, block_...  75 us
    reduce_sum x1, other arithmetic, cross_spectra(): real_part = jnp.sum(own_real * far_real + own_imag * far_imag, axis=0)  13.6 us
    dot_general x1, matrix products, shards(): jnp.dot(partial_value.reshape(-1, 2 * BINS), lag_matrix, precision=lax.Pr...  13.5 us
    ppermute x2, waiting for transfers between devices, shifted(): return lax.ppermute(value, axis, pairs)  12.3 us
    broadcast_in_dim x1, other arithmetic, shards(): return result[None]  5.48 us
    cos x1, other arithmetic, dft_table(): return jnp.concatenate([jnp.cos(phases), -jnp.sin(phases)], axis=1)  3.14 us
  transfers between devices with their start and end apart: 3, of which 3 were waited for; matrix products, arithmetic and copies ran while one was open for 2% of the time, Pallas kernels for 0%

commit v1 on v0

v1 whole, which is shorter than its diff:
```python
import functools
import math

import jax
import jax.numpy as jnp
import ml_dtypes
import numpy as np
from jax import lax
from jax.experimental import pallas as pl
from jax.experimental.pallas import tpu as pltpu
from jax.sharding import PartitionSpec as P

BINS = 128
HALF_LAG = 64
OFFS = 3
LAGS = 2 * HALF_LAG + 1
WATER_LEVEL = 0.1
EPSILON = 1e-06

LANES = 128
RUN = 16
GROUPS = BINS // RUN
STEP = 8

F32 = jnp.float32
BF16 = jnp.bfloat16


def dft_tables(samples):
    phase = (np.arange(samples)[:, None] * np.arange(1, BINS + 1)[None, :]) % samples
    phase = phase * (2.0 * math.pi / samples)
    table = np.concatenate([np.cos(phase), -np.sin(phase)], axis=1)
    high = table.astype(ml_dtypes.bfloat16)
    low = (table - high.astype(np.float64)).astype(ml_dtypes.bfloat16)
    return high, low


def lag_table(samples, total_windows):
    lags = np.arange(-HALF_LAG, HALF_LAG + 1)
    phase = (np.arange(1, BINS + 1)[:, None] * lags[None, :]) % samples
    phase = phase * (2.0 * math.pi / samples)
    table = np.concatenate([np.cos(phase), -np.sin(phase)], axis=0)
    return (table / math.sqrt(BINS * total_windows)).astype(ml_dtypes.bfloat16)


def spectra_kernel(first_ref, dead_ref, trace_ref, high_ref, low_ref, out_ref):
    windows, channels, samples = trace_ref.shape
    traces = trace_ref[...].reshape(windows * channels, samples)
    high = traces.astype(BF16)
    low = (traces - high.astype(F32)).astype(BF16)
    dot = functools.partial(jnp.dot, preferred_element_type=F32)
    raw = dot(high, high_ref[...]) + dot(low, high_ref[...]) + dot(high, low_ref[...])
    ids = first_ref[0] + lax.broadcasted_iota(jnp.int32, (channels, 1), 0)
    dead = jnp.where(ids == dead_ref[...], 1.0, 0.0)
    live = 1.0 - jnp.max(dead, axis=1, keepdims=True)
    parts = []
    for window in range(windows):
        rows = slice(window * channels, (window + 1) * channels)
        real, imag = raw[rows, :BINS], raw[rows, BINS:]
        power = real * real + imag * imag
        mean = jnp.sum(power, axis=1, keepdims=True) * (1.0 / BINS)
        factor = lax.rsqrt(power + WATER_LEVEL * mean + EPSILON) * live
        parts += [real * factor, imag * factor]
    run_of = lax.broadcasted_iota(jnp.int32, (1, LANES), 1) // RUN
    for bit in (1, 2, 4):
        keep = (run_of & bit) == 0
        for index in range(len(parts)):
            if index & bit:
                continue
            first, second = parts[index], parts[index | bit]
            parts[index] = jnp.where(keep, first, pltpu.roll(second, bit * RUN, 1))
            parts[index | bit] = jnp.where(keep, pltpu.roll(first, LANES - bit * RUN, 1), second)
    for group, part in enumerate(parts):
        out_ref[:, group * LANES : (group + 1) * LANES] = part.astype(BF16)


def block_spectra(traces, dead_channels, first_channel):
    windows, channels, samples = traces.shape
    assert 2 * windows == LANES // RUN and GROUPS == 2 * windows
    high, low = dft_tables(samples)
    vmem = pl.BlockSpec(memory_space=pltpu.VMEM)
    return pl.pallas_call(
        spectra_kernel,
        out_shape=jax.ShapeDtypeStruct((channels, GROUPS * LANES), BF16),
        in_specs=[pl.BlockSpec(memory_space=pltpu.SMEM), vmem, vmem, vmem, vmem],
        out_specs=vmem,
        name="spectra",
    )(first_channel, dead_channels[None, :], traces, jnp.asarray(high), jnp.asarray(low))


def correlation_kernel(offsets, sources, share, rank_ref, plan_ref, lag_ref, *refs):
    own_refs, refs = refs[:sources], refs[sources:]
    far_refs, refs = refs[: sources * len(offsets)], refs[sources * len(offsets) :]
    out_ref, real_ref, imag_ref, far_ref, cross_ref, lagged_ref, sems = refs[-7:]
    channels = own_refs[0].shape[0]
    columns = len(offsets) * channels
    pairs = sources // 2
    rank = rank_ref[0]
    first_row = rank * share

    run_of = lax.broadcasted_iota(jnp.int32, (1, LANES), 1) // RUN
    even = (run_of & 1) == 0
    for source, own_ref in enumerate(own_refs):
        for group in range(GROUPS):
            lanes = pl.ds(((source // 2) * GROUPS + group) * 2 * LANES + (source % 2) * LANES, LANES)
            value = own_ref[:, group * LANES : (group + 1) * LANES].astype(F32)
            real_ref[:, lanes] = value
            left, right = pltpu.roll(value, LANES - RUN, 1), pltpu.roll(value, RUN, 1)
            imag_ref[:, lanes] = jnp.where(even, left, -right)
    for place in range(len(offsets)):
        for source in range(sources):
            far = far_refs[place * sources + source]
            for group in range(GROUPS):
                far_ref[
                    (source // 2) * GROUPS + group,
                    place * channels : (place + 1) * channels,
                    (source % 2) * LANES : (source % 2 + 1) * LANES,
                ] = far[:, group * LANES : (group + 1) * LANES]

    diagonal = (
        lax.broadcasted_iota(jnp.int32, (RUN, 2 * LANES), 1) % RUN
        == lax.broadcasted_iota(jnp.int32, (RUN, 2 * LANES), 0)
    )
    column = lax.broadcasted_iota(jnp.int32, (1, columns), 1)
    weight = jnp.full((1, columns), plan_ref[0, offsets[-1]].astype(F32))
    for place in range(len(offsets) - 1):
        here = plan_ref[0, offsets[place]].astype(F32)
        weight = jnp.where(column // channels == place, here, weight)
    lags = lag_ref[...]

    def copy(step):
        return pltpu.make_async_copy(
            lagged_ref.at[step],
            out_ref.at[0, pl.ds(step * STEP, STEP), pl.ds(offsets[0], len(offsets))],
            sems.at[step],
        )

    def one_step(step, carry):
        for group in range(GROUPS):
            total = None
            for pair in range(pairs):
                blocks = []
                lanes = pl.ds((pair * GROUPS + group) * 2 * LANES, 2 * LANES)
                for row in range(STEP):
                    for ref in (real_ref, imag_ref):
                        one = ref[pl.ds(first_row + step * STEP + row, 1), lanes]
                        spread = jnp.broadcast_to(one, (RUN, 2 * LANES))
                        blocks.append(jnp.where(diagonal, spread, 0.0).astype(BF16))
                near = jnp.concatenate(blocks, axis=0)
                term = lax.dot_general(
                    near,
                    far_ref[pair * GROUPS + group],
                    (((1,), (1,)), ((), ())),
                    preferred_element_type=F32,
                )
                total = term if total is None else total + term
            for row in range(STEP):
                scale = weight
                if offsets[0] == 0:
                    above = column > first_row + step * STEP + row
                    scale = jnp.where(jnp.logical_or(above, column >= channels), weight, 0.0)
                for part in range(2):
                    at = (2 * row + part) * RUN
                    cross_ref[row, part * BINS + group * RUN : part * BINS + (group + 1) * RUN, :] = (
                        total[at : at + RUN] * scale
                    ).astype(BF16)
        for row in range(STEP):
            lagged = lax.dot_general(
                cross_ref[row], lags, (((0,), (0,)), ((), ())), preferred_element_type=F32
            )
            for place in range(len(offsets)):
                lagged_ref[step, row, place] = lagged[place * channels : (place + 1) * channels]
        copy(step).start()
        return carry

    steps = share // STEP
    lax.fori_loop(0, steps, one_step, 0)
    for step in range(steps):
        copy(step).wait()


def correlate(offsets, rank, plan, samples, own, far, share, total_windows, previous=None):
    sources = len(own)
    channels = own[0].shape[0]
    count = len(offsets)
    pairs = sources // 2
    vmem = pl.BlockSpec(memory_space=pltpu.VMEM)
    smem = pl.BlockSpec(memory_space=pltpu.SMEM)
    hbm = pl.BlockSpec(memory_space=pl.ANY)
    arrays = [rank, plan, jnp.asarray(lag_table(samples, total_windows)), *own, *far]
    in_specs = [smem, smem] + [vmem] * (len(arrays) - 2)
    aliases = {}
    if previous is not None:
        aliases = {len(arrays): 0}
        arrays.append(previous)
        in_specs.append(hbm)
    steps = share // STEP
    return pl.pallas_call(
        functools.partial(correlation_kernel, offsets, sources, share),
        out_shape=jax.ShapeDtypeStruct((1, share, OFFS, channels, LAGS), F32),
        in_specs=in_specs,
        out_specs=hbm,
        scratch_shapes=[
            pltpu.VMEM((channels, pairs * GROUPS * 2 * LANES), F32),
            pltpu.VMEM((channels, pairs * GROUPS * 2 * LANES), F32),
            pltpu.VMEM((pairs * GROUPS, count * channels, 2 * LANES), BF16),
            pltpu.VMEM((STEP, 2 * BINS, count * channels), BF16),
            pltpu.VMEM((steps, STEP, count, channels, LAGS), F32),
            pltpu.SemaphoreType.DMA((steps,)),
        ],
        input_output_aliases=aliases,
        cost_estimate=pl.CostEstimate(
            flops=2 * share * 2 * BINS * 2 * LANES * pairs * channels * count,
            bytes_accessed=share * count * channels * 2 * LANES * 4,
            transcendentals=0,
        ),
        name="correlate_" + "_".join(str(offset) for offset in offsets),
    )(*arrays)


def moved(value, blocks, ranks):
    block_count, rank_count = lax.axis_size("chan"), lax.axis_size("tm")
    pairs = []
    for block in range(block_count):
        for rank in range(rank_count):
            to = ((block + blocks) % block_count) * rank_count + (rank + ranks) % rank_count
            pairs.append((block * rank_count + rank, to))
    return lax.ppermute(value, ("chan", "tm"), pairs)


def shards(traces, plan, dead_channels):
    windows, channels, samples = traces.shape
    ranks = lax.axis_size("tm")
    share = channels // ranks
    assert ranks % 2 == 0 and share % STEP == 0
    first_channel = (lax.axis_index("chan") * channels).astype(jnp.int32).reshape(1)
    rank = lax.axis_index("tm").astype(jnp.int32).reshape(1)
    mine = block_spectra(traces, dead_channels, first_channel)
    blocks = [
        [mine if (offset, step) == (0, 0) else moved(mine, offset, step) for step in range(ranks)]
        for offset in range(OFFS)
    ]
    own = blocks[0]
    run = functools.partial(
        correlate,
        rank=rank,
        plan=plan,
        samples=samples,
        own=own,
        share=share,
        total_windows=windows * ranks,
    )
    result = run((0,), far=own)
    return run((1, 2), far=blocks[1] + blocks[2], previous=result)


def solution(mesh):
    in_specs = (P("tm", "chan", None), P("chan", None), P())
    out_specs = P("chan", "tm", None, None, None)
    return jax.shard_map(shards, mesh=mesh, in_specs=in_specs, out_specs=out_specs, check_vma=False)
```

time: 145 us -> 27.2 us (0.19)
  waiting for transfers between devices: 87.3 us -> 3.08 us
  other arithmetic: 27.4 us -> 0 us
  matrix products: 15.1 us -> 0 us
  Pallas kernels: 0 us -> 14.1 us
  between operations: 13.5 us -> 0.04 us
  starting transfers between devices: 0.55 us -> 8.54 us
    reduce_scatter x1 -> x0, waiting for transfers between devices: 75 us -> none  [shards(): lax.psum_scatter(lagged.reshape(lax.axis_size('tm') * share, OFFS, block_...]
    dot_general x2 -> x0, matrix products: 15.1 us -> none  [the longest x1 13.5 us: shards(): jnp.dot(partial_value.reshape(-1, 2 * BINS), lag_matrix, precision=lax.Pr...]
    pallas_call x0 -> x3, Pallas kernels: none -> 14.1 us  [the longest x2 10.5 us: correlate(): pl.pallas_call(functools.partial(correlation_kernel, offsets, sources, sh...]
    reduce_sum x2 -> x0, other arithmetic: 13.7 us -> none  [the longest x1 13.6 us: cross_spectra(): real_part = jnp.sum(own_real * far_real + own_imag * far_imag, axis=0)]
    ppermute x2 -> x5, waiting for transfers between devices: 12.3 us -> 3.08 us  [moved(): return lax.ppermute(value, ('chan', 'tm'), pairs)]
    ppermute x2 -> x5, starting transfers between devices: 0.55 us -> 8.54 us  [moved(): return lax.ppermute(value, ('chan', 'tm'), pairs)]
    broadcast_in_dim x1 -> x0, other arithmetic: 5.48 us -> none  [shards(): return result[None]]
    cos x2 -> x0, other arithmetic: 4.16 us -> none  [the longest x1 3.14 us: dft_table(): return jnp.concatenate([jnp.cos(phases), -jnp.sin(phases)], axis=1)]
  transfers between devices with their start and end apart: 3 -> 5, of which waited for: 3 -> 3; matrix products, arithmetic and copies ran while one was open for 2% -> 0% of each run, Pallas kernels for 0% -> 19%
where the time goes in v1:
time: 27.2 us; the launch traced here: 27.1 us
  Pallas kernels  14.1 us (52%)
  starting transfers between devices  8.54 us (31%)
  waiting for transfers between devices  3.08 us (11%)
  local copies, waits for them, and re-layouts  1.3 us (5%)
    pallas_call x2, Pallas kernels, correlate(): pl.pallas_call(functools.partial(correlation_kernel, offsets, sources, sh...  10.5 us
    ppermute x5, starting transfers between devices, moved(): return lax.ppermute(value, ('chan', 'tm'), pairs)  8.54 us
    pallas_call x1, Pallas kernels, block_spectra(): pl.pallas_call(spectra_kernel, out_shape=jax.ShapeDtypeStruct((channels,...  3.59 us
    ppermute x5, waiting for transfers between devices, moved(): return lax.ppermute(value, ('chan', 'tm'), pairs)  3.08 us
    unnamed x10, local copies, waits for them, and re-layouts  1.3 us
  transfers between devices with their start and end apart: 5, of which 3 were waited for; matrix products, arithmetic and copies ran while one was open for 0% of the time, Pallas kernels for 19%

profile of v1, /device:TPU:0, one launch (start us, length us, event | category | flops | bytes accessed | tf_op | source)
XLA Modules:
  0.0 27.1 jit_solution(3810377080361275310)
XLA Ops:
  0.0 3.6 %spectra.1.refs_0_.refs_2_ = bf16[64,1024]{1,0:T(8,128)(2,1)} custom-call(s32[1]{0:T(128)} %bitcast.1.first_ref, s32[1,96]{1,0:T(1,128)} %bitcast.3, f32[4,64,1500]{2,1,0:T(8,128)} %trace_ref.1, bf16[1500,256]{1,0:T(8,128)(2,1)} %constant.16.clone.high_ref, bf16[1500,256]{1,0:T(8,128)(2,1)} %constant.17.clone.low_ref), custom_call_target="tpu_custom_call" | custom-call | tf_op jit(solution)/shard_map/spectra/pallas_call | solution.py:82
  3.6 3.0 %collective-permute-start = (bf16[64,1024]{1,0:T(8,128)(2,1)}, bf16[64,1024]{1,0:T(8,128)(2,1)S(1)}, u32[]{:S(2)}, u32[]{:S(2)}) collective-permute-start(bf16[64,1024]{1,0:T(8,128)(2,1)} %spectra.1.refs_0_.refs_2_), channel_id=1, source_target_pairs={{0,1},{1,0},{2,3},{3,2},{4,5},{5,4},{6,7},{7,6},{8,9},{9,8},{10,11... | collective-permute-start | bytes 393224 | tf_op jit(solution)/shard_map/ppermute | solution.py:228
  6.6 1.5 %collective-permute-start.4 = (bf16[64,1024]{1,0:T(8,128)(2,1)}, bf16[64,1024]{1,0:T(8,128)(2,1)S(1)}, u32[]{:S(2)}, u32[]{:S(2)}) collective-permute-start(bf16[64,1024]{1,0:T(8,128)(2,1)} %spectra.1.refs_0_.refs_2_), channel_id=1, source_target_pairs={{0,5},{1,4},{2,7},{3,6},{4,9},{5,8},{6,11},{7,10},{8,13},{9,12},{1... | collective-permute-start | bytes 393224 | tf_op jit(solution)/shard_map/ppermute | solution.py:228
  8.0 1.5 %collective-permute-start.3 = (bf16[64,1024]{1,0:T(8,128)(2,1)}, bf16[64,1024]{1,0:T(8,128)(2,1)S(1)}, u32[]{:S(2)}, u32[]{:S(2)}) collective-permute-start(bf16[64,1024]{1,0:T(8,128)(2,1)} %spectra.1.refs_0_.refs_2_), channel_id=1, source_target_pairs={{0,4},{1,5},{2,6},{3,7},{4,8},{5,9},{6,10},{7,11},{8,12},{9,13},{1... | collective-permute-start | bytes 393224 | tf_op jit(solution)/shard_map/ppermute | solution.py:228
  9.6 0.1 collective-permute-start.2
  9.7 2.5 %collective-permute-start.1 = (bf16[64,1024]{1,0:T(8,128)(2,1)}, bf16[64,1024]{1,0:T(8,128)(2,1)S(1)}, u32[]{:S(2)}, u32[]{:S(2)}) collective-permute-start(bf16[64,1024]{1,0:T(8,128)(2,1)} %spectra.1.refs_0_.refs_2_), channel_id=1, source_target_pairs={{0,2},{1,3},{2,4},{3,5},{4,6},{5,7},{6,8},{7,9},{8,10},{9,11},{10,... | collective-permute-start | bytes 393224 | tf_op jit(solution)/shard_map/ppermute | solution.py:228
  12.1 0.0 collective-permute-done.refs_1_.refs_3_
  12.1 0.0 copy-start
  12.1 0.7 %copy-done = bf16[64,1024]{1,0:T(8,128)(2,1)} copy-done((bf16[64,1024]{1,0:T(8,128)(2,1)}, bf16[64,1024]{1,0:T(8,128)(2,1)S(1)}, u32[]{:S(2)}) %copy-start) | copy-done | bytes 131096
  12.8 5.0 %correlate_0.1.refs_6_ = f32[1,32,3,64,129]{4,3,2,1,0:T(8,128)} custom-call(s32[1]{0:T(128)} %bitcast.rank_ref, s32[1,3]{1,0:T(1,128)} %plan_ref.3, bf16[256,129]{1,0:T(8,128)(2,1)} %constant.18.clone.lag_ref, bf16[64,1024]{1,0:T(8,128)(2,1)} %spectra.1.refs_0_.refs_2_, bf16[64,1024]{1,0:T(8,128)(2,1)} %copy-done, bf16[64,1024]{1,0:T(8,128)(2,1)} %spectra.1.refs_0_.refs_2_, ...), custom_call_target="tpu_custom_call" | custom-call | flops 268435456 | bytes 2097152 | tf_op jit(solution)/shard_map/correlate_0/pallas_call | solution.py:198
  17.8 0.0 collective-permute-done.4.refs_5_
  17.9 0.0 copy-start.1
  17.9 1.1 %collective-permute-done.3.refs_4_ = bf16[64,1024]{1,0:T(8,128)(2,1)S(1)} collective-permute-done((bf16[64,1024]{1,0:T(8,128)(2,1)}, bf16[64,1024]{1,0:T(8,128)(2,1)S(1)}, u32[]{:S(2)}, u32[]{:S(2)}) %collective-permute-start.3) | collective-permute-done | bytes 131104 | tf_op jit(solution)/shard_map/ppermute | solution.py:228
  19.0 0.0 copy-start.2
  19.0 1.3 %collective-permute-done.2.refs_3_ = bf16[64,1024]{1,0:T(8,128)(2,1)S(1)} collective-permute-done((bf16[64,1024]{1,0:T(8,128)(2,1)}, bf16[64,1024]{1,0:T(8,128)(2,1)S(1)}, u32[]{:S(2)}, u32[]{:S(2)}) %collective-permute-start.2) | collective-permute-done | bytes 131104 | tf_op jit(solution)/shard_map/ppermute | solution.py:228
  20.3 0.0 copy-start.3
  20.3 0.7 %collective-permute-done.1.refs_2_ = bf16[64,1024]{1,0:T(8,128)(2,1)S(1)} collective-permute-done((bf16[64,1024]{1,0:T(8,128)(2,1)}, bf16[64,1024]{1,0:T(8,128)(2,1)S(1)}, u32[]{:S(2)}, u32[]{:S(2)}) %collective-permute-start.1) | collective-permute-done | bytes 131104 | tf_op jit(solution)/shard_map/ppermute | solution.py:228
  20.9 0.0 copy-done.1
  20.9 0.0 copy-done.2
  20.9 0.0 copy-done.3
  21.0 0.0 copy-start.4
  21.0 0.6 %copy-done.4 = bf16[64,1024]{1,0:T(8,128)(2,1)} copy-done((bf16[64,1024]{1,0:T(8,128)(2,1)}, bf16[64,1024]{1,0:T(8,128)(2,1)S(1)}, u32[]{:S(2)}) %copy-start.4) | copy-done | bytes 131096
  21.6 5.5 %correlate_1_2.1 = f32[1,32,3,64,129]{4,3,2,1,0:T(8,128)} custom-call(s32[1]{0:T(128)} %bitcast.rank_ref, s32[1,3]{1,0:T(1,128)} %plan_ref.3, bf16[256,129]{1,0:T(8,128)(2,1)} %constant.18.clone.lag_ref, bf16[64,1024]{1,0:T(8,128)(2,1)} %spectra.1.refs_0_.refs_2_, bf16[64,1024]{1,0:T(8,128)(2,1)} %copy-done, ...), custom_call_target="tpu_custom_call", output_to_operand_aliasing={{}: (9, {})} | custom-call | flops 536870912 | bytes 4194304 | tf_op jit(solution)/shard_map/correlate_1_2/pallas_call | solution.py:198
Async XLA Ops:
  3.6 8.5 %collective-permute-start = (bf16[64,1024]{1,0:T(8,128)(2,1)}, bf16[64,1024]{1,0:T(8,128)(2,1)S(1)}, u32[]{:S(2)}, u32[]{:S(2)}) collective-permute-start(bf16[64,1024]{1,0:T(8,128)(2,1)} %spectra.1.refs_0_.refs_2_), channel_id=1, source_target_pairs={{0,1},{1,0},{2,3},{3,2},{4,5},{5,4},{6,7},{7,6},{8,9},{9,8},{10,11... | collective-permute-start | bytes 393224 | tf_op jit(solution)/shard_map/ppermute | solution.py:228
  6.6 11.3 %collective-permute-start.4 = (bf16[64,1024]{1,0:T(8,128)(2,1)}, bf16[64,1024]{1,0:T(8,128)(2,1)S(1)}, u32[]{:S(2)}, u32[]{:S(2)}) collective-permute-start(bf16[64,1024]{1,0:T(8,128)(2,1)} %spectra.1.refs_0_.refs_2_), channel_id=1, source_target_pairs={{0,5},{1,4},{2,7},{3,6},{4,9},{5,8},{6,11},{7,10},{8,13},{9,12},{1... | collective-permute-start | bytes 393224 | tf_op jit(solution)/shard_map/ppermute | solution.py:228
  8.0 10.9 %collective-permute-start.3 = (bf16[64,1024]{1,0:T(8,128)(2,1)}, bf16[64,1024]{1,0:T(8,128)(2,1)S(1)}, u32[]{:S(2)}, u32[]{:S(2)}) collective-permute-start(bf16[64,1024]{1,0:T(8,128)(2,1)} %spectra.1.refs_0_.refs_2_), channel_id=1, source_target_pairs={{0,4},{1,5},{2,6},{3,7},{4,8},{5,9},{6,10},{7,11},{8,12},{9,13},{1... | collective-permute-start | bytes 393224 | tf_op jit(solution)/shard_map/ppermute | solution.py:228
  9.6 10.7 %collective-permute-start.2 = (bf16[64,1024]{1,0:T(8,128)(2,1)}, bf16[64,1024]{1,0:T(8,128)(2,1)S(1)}, u32[]{:S(2)}, u32[]{:S(2)}) collective-permute-start(bf16[64,1024]{1,0:T(8,128)(2,1)} %spectra.1.refs_0_.refs_2_), channel_id=1, source_target_pairs={{0,3},{1,2},{2,5},{3,4},{4,7},{5,6},{6,9},{7,8},{8,11},{9,10},{10,... | collective-permute-start | bytes 393224 | tf_op jit(solution)/shard_map/ppermute | solution.py:228
  9.7 11.3 %collective-permute-start.1 = (bf16[64,1024]{1,0:T(8,128)(2,1)}, bf16[64,1024]{1,0:T(8,128)(2,1)S(1)}, u32[]{:S(2)}, u32[]{:S(2)}) collective-permute-start(bf16[64,1024]{1,0:T(8,128)(2,1)} %spectra.1.refs_0_.refs_2_), channel_id=1, source_target_pairs={{0,2},{1,3},{2,4},{3,5},{4,6},{5,7},{6,8},{7,9},{8,10},{9,11},{10,... | collective-permute-start | bytes 393224 | tf_op jit(solution)/shard_map/ppermute | solution.py:228
  12.1 0.7 %copy-start = (bf16[64,1024]{1,0:T(8,128)(2,1)}, bf16[64,1024]{1,0:T(8,128)(2,1)S(1)}, u32[]{:S(2)}) copy-start(bf16[64,1024]{1,0:T(8,128)(2,1)S(1)} %collective-permute-done.refs_1_.refs_3_) | copy-start | bytes 393220
  17.9 3.1 %copy-start.1 = (bf16[64,1024]{1,0:T(8,128)(2,1)}, bf16[64,1024]{1,0:T(8,128)(2,1)S(1)}, u32[]{:S(2)}) copy-start(bf16[64,1024]{1,0:T(8,128)(2,1)S(1)} %collective-permute-done.4.refs_5_) | copy-start | bytes 393220
  19.0 2.0 %copy-start.2 = (bf16[64,1024]{1,0:T(8,128)(2,1)}, bf16[64,1024]{1,0:T(8,128)(2,1)S(1)}, u32[]{:S(2)}) copy-start(bf16[64,1024]{1,0:T(8,128)(2,1)S(1)} %collective-permute-done.3.refs_4_) | copy-start | bytes 393220
  20.3 0.7 %copy-start.3 = (bf16[64,1024]{1,0:T(8,128)(2,1)}, bf16[64,1024]{1,0:T(8,128)(2,1)S(1)}, u32[]{:S(2)}) copy-start(bf16[64,1024]{1,0:T(8,128)(2,1)S(1)} %collective-permute-done.2.refs_3_) | copy-start | bytes 393220
  21.0 0.6 %copy-start.4 = (bf16[64,1024]{1,0:T(8,128)(2,1)}, bf16[64,1024]{1,0:T(8,128)(2,1)S(1)}, u32[]{:S(2)}) copy-start(bf16[64,1024]{1,0:T(8,128)(2,1)S(1)} %collective-permute-done.1.refs_2_) | copy-start | bytes 393220

commit v2 on v1

v2 whole, which is shorter than its diff:
```python
import functools
import math

import jax
import jax.numpy as jnp
import ml_dtypes
import numpy as np
from jax import lax
from jax.experimental import pallas as pl
from jax.experimental.pallas import tpu as pltpu
from jax.sharding import PartitionSpec as P

BINS = 128
HALF_LAG = 64
OFFS = 3
LAGS = 2 * HALF_LAG + 1
WATER_LEVEL = 0.1
EPSILON = 1e-06

LANES = 128
RUN = 16
GROUPS = BINS // RUN
STEP = 16
BATCH = 8
SEGMENT = 256
VMEM_LIMIT = 24 << 20
MERGED = False

F32 = jnp.float32
BF16 = jnp.bfloat16


def dft_tables(samples):
    bins = np.arange(1, BINS + 1)[None, :]
    phase = np.arange(SEGMENT)[:, None] * bins % samples * (2.0 * math.pi / samples)
    table = np.concatenate([np.cos(phase), -np.sin(phase)], axis=1)
    high = table.astype(ml_dtypes.bfloat16)
    low = (table - high.astype(np.float64)).astype(ml_dtypes.bfloat16)
    starts = np.arange(0, samples, SEGMENT)[:, None]
    turn = starts * bins % samples * (2.0 * math.pi / samples)
    turns = np.concatenate([np.cos(turn), -np.sin(turn)], axis=1).astype(np.float32)
    return high, low, turns


def lag_table(samples, total_windows):
    lags = np.arange(-HALF_LAG, HALF_LAG + 1)
    phase = (np.arange(1, BINS + 1)[:, None] * lags[None, :]) % samples
    phase = phase * (2.0 * math.pi / samples)
    table = np.concatenate([np.cos(phase), -np.sin(phase)], axis=0)
    return (table / math.sqrt(BINS * total_windows)).astype(ml_dtypes.bfloat16)


def spectra_kernel(first_ref, *refs):
    hbm, (out_ref, weight_ref, lag_ref), places, (tail_ref, sems) = refs[:7], refs[7:10], refs[10:16], refs[16:]
    places = (*places, lag_ref)
    trace_hbm, held_ref = hbm[0], places[0]
    dead_ref, plan_ref, high_ref, low_ref, turn_ref = places[1:6]
    windows, channels, samples = trace_hbm.shape

    def copy(window):
        return pltpu.make_async_copy(trace_hbm.at[window], held_ref.at[window], sems.at[window])

    small = [
        pltpu.make_async_copy(source, place, sems.at[windows + index])
        for index, (source, place) in enumerate(zip(hbm[1:], places[1:], strict=True))
    ]
    for one in (small[2], small[3]):
        one.start()
    for window in range(windows):
        copy(window).start()
    for one in (*small[:2], *small[4:]):
        one.start()
    dot = functools.partial(jnp.dot, preferred_element_type=F32)
    segments = pl.cdiv(samples, SEGMENT)
    last = samples - (segments - 1) * SEGMENT
    tail_ref[...] = jnp.zeros_like(tail_ref)
    small[2].wait()
    small[3].wait()
    high_table, low_table = high_ref[...], low_ref[...]
    reals, imags = [], []
    live = None
    for window in range(windows):
        copy(window).wait()
        tail_ref[:, :last] = held_ref[window, :, samples - last : samples]
        highs, lows = [], []
        for segment in range(segments):
            if segment == segments - 1:
                piece = tail_ref[...]
            else:
                piece = held_ref[window, :, segment * SEGMENT : (segment + 1) * SEGMENT]
            highs.append(piece.astype(BF16))
            lows.append((piece - highs[-1].astype(F32)).astype(BF16))
        high = jnp.concatenate(highs, axis=0)
        low = jnp.concatenate(lows, axis=0)
        all_raw = dot(high, high_table) + dot(low, high_table) + dot(high, low_table)
        if window == 0:
            for one in (*small[:2], *small[4:]):
                one.wait()
            ids = first_ref[0] + lax.broadcasted_iota(jnp.int32, (channels, 1), 0)
            dead = jnp.where(ids == dead_ref[...], 1.0, 0.0)
            live = 1.0 - jnp.max(dead, axis=1, keepdims=True)
            weight_ref[...] = jnp.zeros_like(weight_ref)
            for offset in range(OFFS):
                weight = plan_ref[:, offset : offset + 1].astype(F32)
                weight_ref[offset : offset + 1, :] = jnp.broadcast_to(weight, (1, LANES))
        real = imag = None
        for segment in range(segments):
            raw = all_raw[segment * channels : (segment + 1) * channels]
            if segment == 0:
                real, imag = raw[:, :BINS], raw[:, BINS:]
            else:
                cosine = turn_ref[segment : segment + 1, :BINS]
                sine = turn_ref[segment : segment + 1, BINS:]
                real += raw[:, :BINS] * cosine - raw[:, BINS:] * sine
                imag += raw[:, BINS:] * cosine + raw[:, :BINS] * sine
        power = real * real + imag * imag
        mean = jnp.sum(power, axis=1, keepdims=True) * (1.0 / BINS)
        factor = lax.rsqrt(power + WATER_LEVEL * mean + EPSILON) * live
        reals.append(real * factor)
        imags.append(imag * factor)
    parts = reals + imags
    run_of = lax.broadcasted_iota(jnp.int32, (1, LANES), 1) // RUN
    for bit in (1, 2, 4):
        keep = (run_of & bit) == 0
        for index in range(len(parts)):
            if index & bit:
                continue
            first, second = parts[index], parts[index | bit]
            parts[index] = jnp.where(keep, first, pltpu.roll(second, bit * RUN, 1))
            parts[index | bit] = jnp.where(keep, pltpu.roll(first, LANES - bit * RUN, 1), second)
    for group, part in enumerate(parts):
        out_ref[:, group * LANES : (group + 1) * LANES] = part.astype(BF16)


def block_spectra(traces, dead_channels, plan, first_channel, total_windows):
    windows, channels, samples = traces.shape
    assert 2 * windows == LANES // RUN and GROUPS == 2 * windows
    high, low, turns = (jnp.asarray(table) for table in dft_tables(samples))
    lags = jnp.asarray(lag_table(samples, total_windows))
    arrays = [traces, dead_channels[None, :], plan, high, low, turns, lags]
    arrays = [pltpu.with_memory_space_constraint(array, pltpu.HBM) for array in arrays]
    vmem = pl.BlockSpec(memory_space=pltpu.VMEM)
    return pl.pallas_call(
        spectra_kernel,
        out_shape=[
            jax.ShapeDtypeStruct((channels, GROUPS * LANES), BF16),
            jax.ShapeDtypeStruct((8, LANES), F32),
            jax.ShapeDtypeStruct(lags.shape, lags.dtype),
        ],
        in_specs=[pl.BlockSpec(memory_space=pltpu.SMEM)]
        + [pl.BlockSpec(memory_space=pltpu.HBM)] * len(arrays),
        out_specs=[vmem] * 3,
        scratch_shapes=[pltpu.VMEM(array.shape, array.dtype) for array in arrays[:-1]]
        + [
            pltpu.VMEM((channels, SEGMENT), F32),
            pltpu.SemaphoreType.DMA((windows + len(arrays) - 1,)),
        ],
        compiler_params=pltpu.CompilerParams(vmem_limit_bytes=VMEM_LIMIT),
        name="spectra",
    )(first_channel, *arrays)


def correlation_kernel(offsets, sources, share, step_rows, rank_ref, weight_ref, lag_ref, *refs):
    own_refs, refs = refs[:sources], refs[sources:]
    far_refs, refs = refs[: sources * len(offsets)], refs[sources * len(offsets) :]
    out_ref, near_ref, far_ref, cross_ref, lagged_ref, sems = refs[-6:]
    channels = own_refs[0].shape[0]
    columns = len(offsets) * channels
    pairs = sources // 2
    first_row = rank_ref[0] * share

    def lanes_of(source, group):
        start = ((source // 2) * GROUPS + group) * 2 * LANES + (source % 2) * LANES
        return slice(start, start + LANES)

    held_first = first_row
    for source, own_ref in enumerate(own_refs):
        for group in range(GROUPS):
            at = slice(group * LANES, (group + 1) * LANES)
            if share % 16 == 0:
                value = own_ref[pl.ds(pl.multiple_of(first_row, share), share), at]
                held_first = 0
            else:
                value = own_ref[:, at]
            near_ref[:, lanes_of(source, group)] = value.astype(F32)
    sign = jnp.where(lax.broadcasted_iota(jnp.int32, (1, LANES), 1) < LANES // 2, -1.0, 1.0)
    for place, offset in enumerate(offsets):
        weight = weight_ref[offset : offset + 1, :]
        turned_weight = weight * sign
        rows = slice(place * channels, (place + 1) * channels)
        turned_rows = slice(columns + place * channels, columns + (place + 1) * channels)
        for source in range(sources):
            far = far_refs[place * sources + source]
            lanes = slice((source % 2) * LANES, (source % 2 + 1) * LANES)
            for group in range(GROUPS):
                value = far[:, group * LANES : (group + 1) * LANES].astype(F32)
                turned = pltpu.roll(value, LANES // 2, 1) * turned_weight
                slot = (source // 2) * GROUPS + group
                far_ref[slot, rows, lanes] = (value * weight).astype(BF16)
                far_ref[slot, turned_rows, lanes] = turned.astype(BF16)

    diagonal = (
        lax.broadcasted_iota(jnp.int32, (RUN, 2 * LANES), 1) % RUN
        == lax.broadcasted_iota(jnp.int32, (RUN, 2 * LANES), 0)
    )
    column = lax.broadcasted_iota(jnp.int32, (1, 2 * columns), 1) % channels
    lags = lag_ref[...]

    batch = min(BATCH, step_rows)

    def copy(index):
        return pltpu.make_async_copy(
            lagged_ref.at[index],
            out_ref.at[0, pl.ds(index * batch, batch), pl.ds(offsets[0], len(offsets))],
            sems.at[index],
        )

    def one_step(step, carry):
        for group in range(GROUPS):
            total = None
            for pair in range(pairs):
                blocks = []
                slot = pair * GROUPS + group
                lanes = slice(slot * 2 * LANES, (slot + 1) * 2 * LANES)
                for row in range(step_rows):
                    one = near_ref[pl.ds(held_first + step * step_rows + row, 1), lanes]
                    spread = jnp.broadcast_to(one, (RUN, 2 * LANES))
                    blocks.append(jnp.where(diagonal, spread, 0.0).astype(BF16))
                term = lax.dot_general(
                    jnp.concatenate(blocks, axis=0),
                    far_ref[slot],
                    (((1,), (1,)), ((), ())),
                    preferred_element_type=F32,
                )
                total = term if total is None else total + term
            for row in range(step_rows):
                value = total[row * RUN : (row + 1) * RUN]
                if offsets[0] == 0:
                    value = jnp.where(column > first_row + step * step_rows + row, value, 0.0)
                cross_ref[row, group * RUN : (group + 1) * RUN, :] = value.astype(BF16)
        for start in range(0, step_rows, batch):
            sides = []
            for row in range(start, start + batch):
                cross = cross_ref[row].T
                sides.append(jnp.concatenate([cross[:columns], cross[columns:]], axis=1))
            lagged = jnp.dot(jnp.concatenate(sides, axis=0), lags, preferred_element_type=F32)
            index = (step * step_rows + start) // batch
            lagged_ref[index] = lagged.reshape(batch, len(offsets), channels, LAGS)
            copy(index).start()
        return carry

    lax.fori_loop(0, share // step_rows, one_step, 0)
    for index in range(share // batch):
        copy(index).wait()


def correlate(offsets, rank, weights, lags, own, far, share, previous=None):
    sources = len(own)
    channels = own[0].shape[0]
    count = len(offsets)
    pairs = sources // 2
    vmem = pl.BlockSpec(memory_space=pltpu.VMEM)
    smem = pl.BlockSpec(memory_space=pltpu.SMEM)
    hbm = pl.BlockSpec(memory_space=pltpu.HBM)
    arrays = [rank, weights, lags, *own, *far]
    in_specs = [smem] + [vmem] * (len(arrays) - 1)
    aliases = {}
    if previous is not None:
        aliases = {len(arrays): 0}
        arrays.append(previous)
        in_specs.append(hbm)
    step_rows = min(STEP, share)
    batch = min(BATCH, step_rows)
    held = share if share % 16 == 0 else channels
    return pl.pallas_call(
        functools.partial(correlation_kernel, offsets, sources, share, step_rows),
        out_shape=jax.ShapeDtypeStruct((1, share, OFFS, channels, LAGS), F32),
        in_specs=in_specs,
        out_specs=hbm,
        scratch_shapes=[
            pltpu.VMEM((held, pairs * GROUPS * 2 * LANES), F32),
            pltpu.VMEM((pairs * GROUPS, 2 * count * channels, 2 * LANES), BF16),
            pltpu.VMEM((step_rows, BINS, 2 * count * channels), BF16),
            pltpu.VMEM((share // batch, batch, count, channels, LAGS), F32),
            pltpu.SemaphoreType.DMA((share // batch,)),
        ],
        compiler_params=pltpu.CompilerParams(vmem_limit_bytes=VMEM_LIMIT),
        input_output_aliases=aliases,
        cost_estimate=pl.CostEstimate(
            flops=2 * share * 2 * BINS * 2 * LANES * pairs * channels * count,
            bytes_accessed=share * count * channels * 2 * LANES * 4,
            transcendentals=0,
        ),
        name="correlate_" + "_".join(str(offset) for offset in offsets),
    )(*arrays)


def moved(value, blocks, ranks):
    block_count, rank_count = lax.axis_size("chan"), lax.axis_size("tm")
    pairs = []
    for block in range(block_count):
        for rank in range(rank_count):
            to = ((block + blocks) % block_count) * rank_count + (rank + ranks) % rank_count
            pairs.append((block * rank_count + rank, to))
    return lax.ppermute(value, ("chan", "tm"), pairs)


def swapped(value):
    return lax.ppermute(value, "chan", [(block, block ^ 1) for block in range(lax.axis_size("chan"))])


def shards(traces, plan, dead_channels):
    windows, channels, _ = traces.shape
    ranks = lax.axis_size("tm")
    share = channels // ranks
    assert ranks % 2 == 0 and share % min(STEP, share) == 0
    first_channel = (lax.axis_index("chan") * channels).astype(jnp.int32).reshape(1)
    rank = lax.axis_index("tm").astype(jnp.int32).reshape(1)
    mine, weights, lags = block_spectra(traces, dead_channels, plan, first_channel, windows * ranks)
    behind = [moved(mine, 2, step) for step in reversed(range(ranks))][::-1]
    own = [mine] + [moved(mine, 0, step) for step in range(1, ranks)]
    run = functools.partial(
        correlate, rank=rank, weights=weights, lags=lags, own=own, share=share
    )
    result = run((0,), far=own)
    behind, result = lax.optimization_barrier((behind, result))
    odd = lax.axis_index("chan") % 2 == 1
    beside = [swapped(jnp.where(odd, far, near)) for far, near in zip(behind, own, strict=True)]
    if MERGED:
        return run((1, 2), far=beside + behind, previous=result)
    result = run((2,), far=behind, previous=result)
    return run((1,), far=beside, previous=result)


def solution(mesh):
    in_specs = (P("tm", "chan", None), P("chan", None), P())
    out_specs = P("chan", "tm", None, None, None)
    return jax.shard_map(shards, mesh=mesh, in_specs=in_specs, out_specs=out_specs, check_vma=False)
```

time: 27.2 us -> 24.2 us (0.89)
  waiting for transfers between devices: 3.08 us -> 5.75 us
  Pallas kernels: 14.1 us -> 11.5 us
  starting transfers between devices: 8.54 us -> 6.67 us
  local copies, waits for them, and re-layouts: 1.3 us -> 0 us
    pallas_call x2 -> x3, Pallas kernels: 10.5 us -> 7.77 us  [correlate(): pl.pallas_call(functools.partial(correlation_kernel, offsets, sources, sh...]
    ppermute x5 -> x3, waiting for transfers between devices: 3.08 us -> 5.75 us  [moved(): return lax.ppermute(value, ('chan', 'tm'), pairs)]
    ppermute x5 -> x3, starting transfers between devices: 8.54 us -> 6.04 us  [moved(): return lax.ppermute(value, ('chan', 'tm'), pairs)]
    unnamed x10 -> x0, local copies, waits for them, and re-layouts: 1.3 us -> none
    ppermute x0 -> x2, starting transfers between devices: none -> 0.63 us  [swapped(): lax.ppermute(value, 'chan', [(block, block ^ 1) for block in range(lax.ax...]
  transfers between devices with their start and end apart: 5 -> 5, of which waited for: 3 -> 3; matrix products, arithmetic and copies ran while one was open for 0% -> 0% of each run, Pallas kernels for 19% -> 22%
where the time goes in v2:
time: 24.2 us; the launch traced here: 24 us
  Pallas kernels  11.5 us (48%)
  starting transfers between devices  6.67 us (28%)
  waiting for transfers between devices  5.75 us (24%)
    pallas_call x3, Pallas kernels, correlate(): pl.pallas_call(functools.partial(correlation_kernel, offsets, sources, sh...  7.77 us
    ppermute x3, starting transfers between devices, moved(): return lax.ppermute(value, ('chan', 'tm'), pairs)  6.04 us
    ppermute x3, waiting for transfers between devices, moved(): return lax.ppermute(value, ('chan', 'tm'), pairs)  5.75 us
    pallas_call x1, Pallas kernels, block_spectra(): pl.pallas_call(spectra_kernel, out_shape=[jax.ShapeDtypeStruct((channels,...  3.74 us
    ppermute x2, starting transfers between devices, swapped(): lax.ppermute(value, 'chan', [(block, block ^ 1) for block in range(lax.ax...  0.63 us
  transfers between devices with their start and end apart: 5, of which 3 were waited for; matrix products, arithmetic and copies ran while one was open for 0% of the time, Pallas kernels for 22%

profile of v2, /device:TPU:0, one launch (start us, length us, event | category | flops | bytes accessed | tf_op | source)
XLA Modules:
  0.0 24.0 jit_solution(11271340477371115771)
XLA Ops:
  0.0 3.7 %spectra.1 = (bf16[64,1024]{1,0:T(8,128)(2,1)S(1)}, f32[8,128]{1,0:T(8,128)S(1)}, bf16[256,129]{1,0:T(8,128)(2,1)S(1)}) custom-call(s32[1]{0:T(128)} %bitcast.1.first_ref, f32[4,64,1500]{2,1,0:T(8,128)} %refs_0_.1, s32[1,96]{1,0:T(1,128)} %bitcast.3, s32[1,3]{1,0:T(1,128)} %refs_2_.1, bf16[256,256]{1,0:T(8,128)(2,1)} %constant.32.clone.refs_3_, ...), custom_call_target="tpu_custom_call" | custom-call | tf_op jit(solution)/shard_map/spectra/pallas_call | solution.py:143
  3.8 3.0 %collective-permute-start = (bf16[64,1024]{1,0:T(8,128)(2,1)S(1)}, bf16[64,1024]{1,0:T(8,128)(2,1)S(1)}, u32[]{:S(2)}, u32[]{:S(2)}) collective-permute-start(bf16[64,1024]{1,0:T(8,128)(2,1)S(1)} %get-tuple-element.13.refs_0_.refs_2_), channel_id=1, source_target_pairs={{0,1},{1,0},{2,3},{3,2},{4,5},{5,4},{6,7},{7,6},{8,9},{9,8},{10,11... | collective-permute-start | bytes 393224 | tf_op jit(solution)/shard_map/ppermute | solution.py:305
  6.8 1.5 %collective-permute-start.2 = (bf16[64,1024]{1,0:T(8,128)(2,1)S(1)}, bf16[64,1024]{1,0:T(8,128)(2,1)S(1)}, u32[]{:S(2)}, u32[]{:S(2)}) collective-permute-start(bf16[64,1024]{1,0:T(8,128)(2,1)S(1)} %get-tuple-element.13.refs_0_.refs_2_), channel_id=1, source_target_pairs={{0,5},{1,4},{2,7},{3,6},{4,9},{5,8},{6,11},{7,10},{8,13},{9,12},{1... | collective-permute-start | bytes 393224 | tf_op jit(solution)/shard_map/ppermute | solution.py:305
  8.3 1.5 %collective-permute-start.1 = (bf16[64,1024]{1,0:T(8,128)(2,1)S(1)}, bf16[64,1024]{1,0:T(8,128)(2,1)S(1)}, u32[]{:S(2)}, u32[]{:S(2)}) collective-permute-start(bf16[64,1024]{1,0:T(8,128)(2,1)S(1)} %get-tuple-element.13.refs_0_.refs_2_), channel_id=1, source_target_pairs={{0,4},{1,5},{2,6},{3,7},{4,8},{5,9},{6,10},{7,11},{8,12},{9,13},{1... | collective-permute-start | bytes 393224 | tf_op jit(solution)/shard_map/ppermute | solution.py:305
  9.8 0.9 %collective-permute-done.refs_1_.refs_3_ = bf16[64,1024]{1,0:T(8,128)(2,1)S(1)} collective-permute-done((bf16[64,1024]{1,0:T(8,128)(2,1)S(1)}, bf16[64,1024]{1,0:T(8,128)(2,1)S(1)}, u32[]{:S(2)}, u32[]{:S(2)}) %collective-permute-start) | collective-permute-done | bytes 131104 | tf_op jit(solution)/shard_map/ppermute | solution.py:305
  10.7 2.6 %correlate_0.1.refs_4_ = f32[1,32,3,64,129]{4,3,2,1,0:T(8,128)} custom-call(s32[1]{0:T(128)} %bitcast.rank_ref, f32[8,128]{1,0:T(8,128)S(1)} %get-tuple-element.11.weight_ref, bf16[256,129]{1,0:T(8,128)(2,1)S(1)} %get-tuple-element.12.lag_ref, bf16[64,1024]{1,0:T(8,128)(2,1)S(1)} %get-tuple-element.13.refs_0_.refs_2_, ...), custom_call_target="tpu_custom_call" | custom-call | flops 268435456 | bytes 2097152 | tf_op jit(solution)/shard_map/correlate_0/pallas_call | solution.py:275
  13.3 4.1 %collective-permute-done.2.refs_3_ = bf16[64,1024]{1,0:T(8,128)(2,1)S(1)} collective-permute-done((bf16[64,1024]{1,0:T(8,128)(2,1)S(1)}, bf16[64,1024]{1,0:T(8,128)(2,1)S(1)}, u32[]{:S(2)}, u32[]{:S(2)}) %collective-permute-start.2) | collective-permute-done | bytes 131104 | tf_op jit(solution)/shard_map/ppermute | solution.py:305
  17.4 0.7 %collective-permute-done.1.refs_2_ = bf16[64,1024]{1,0:T(8,128)(2,1)S(1)} collective-permute-done((bf16[64,1024]{1,0:T(8,128)(2,1)S(1)}, bf16[64,1024]{1,0:T(8,128)(2,1)S(1)}, u32[]{:S(2)}, u32[]{:S(2)}) %collective-permute-start.1) | collective-permute-done | bytes 131104 | tf_op jit(solution)/shard_map/ppermute | solution.py:305
  18.2 0.1 collective-permute-start.3
  18.3 0.6 %collective-permute-start.4 = (bf16[64,1024]{1,0:T(8,128)(2,1)S(1)}, bf16[64,1024]{1,0:T(8,128)(2,1)S(1)}, u32[]{:S(2)}, u32[]{:S(2)}) collective-permute-start(bf16[64,1024]{1,0:T(8,128)(2,1)S(1)} %broadcast_select_fusion), channel_id=1, source_target_pairs={{0,2},{2,0},{4,6},{6,4},{8,10},{10,8},{12,14},{14,12},{16,18},{18,... | collective-permute-start | bytes 393224 | tf_op jit(solution)/shard_map/ppermute | solution.py:309
  18.8 2.6 %correlate_2.1.refs_4_ = f32[1,32,3,64,129]{4,3,2,1,0:T(8,128)} custom-call(s32[1]{0:T(128)} %bitcast.rank_ref, f32[8,128]{1,0:T(8,128)S(1)} %get-tuple-element.11.weight_ref, bf16[256,129]{1,0:T(8,128)(2,1)S(1)} %get-tuple-element.12.lag_ref, bf16[64,1024]{1,0:T(8,128)(2,1)S(1)} %get-tuple-element.13.refs_0_.refs_2_, ...), custom_call_target="tpu_custom_call", output_to_operand_aliasing={{}: (7, {})} | custom-call | flops 268435456 | bytes 2097152 | tf_op jit(solution)/shard_map/correlate_2/pallas_call | solution.py:275
  21.4 0.0 collective-permute-done.3.refs_2_
  21.4 0.0 collective-permute-done.4.refs_3_
  21.4 2.6 %correlate_1.1 = f32[1,32,3,64,129]{4,3,2,1,0:T(8,128)} custom-call(s32[1]{0:T(128)} %bitcast.rank_ref, f32[8,128]{1,0:T(8,128)S(1)} %get-tuple-element.11.weight_ref, bf16[256,129]{1,0:T(8,128)(2,1)S(1)} %get-tuple-element.12.lag_ref, bf16[64,1024]{1,0:T(8,128)(2,1)S(1)} %get-tuple-element.13.refs_0_.refs_2_, ...), custom_call_target="tpu_custom_call", output_to_operand_aliasing={{}: (7, {})} | custom-call | flops 268435456 | bytes 2097152 | tf_op jit(solution)/shard_map/correlate_1/pallas_call | solution.py:275
  (2 shorter events, 0.0 us)
Async XLA Ops:
  3.8 6.9 %collective-permute-start = (bf16[64,1024]{1,0:T(8,128)(2,1)S(1)}, bf16[64,1024]{1,0:T(8,128)(2,1)S(1)}, u32[]{:S(2)}, u32[]{:S(2)}) collective-permute-start(bf16[64,1024]{1,0:T(8,128)(2,1)S(1)} %get-tuple-element.13.refs_0_.refs_2_), channel_id=1, source_target_pairs={{0,1},{1,0},{2,3},{3,2},{4,5},{5,4},{6,7},{7,6},{8,9},{9,8},{10,11... | collective-permute-start | bytes 393224 | tf_op jit(solution)/shard_map/ppermute | solution.py:305
  6.8 10.6 %collective-permute-start.2 = (bf16[64,1024]{1,0:T(8,128)(2,1)S(1)}, bf16[64,1024]{1,0:T(8,128)(2,1)S(1)}, u32[]{:S(2)}, u32[]{:S(2)}) collective-permute-start(bf16[64,1024]{1,0:T(8,128)(2,1)S(1)} %get-tuple-element.13.refs_0_.refs_2_), channel_id=1, source_target_pairs={{0,5},{1,4},{2,7},{3,6},{4,9},{5,8},{6,11},{7,10},{8,13},{9,12},{1... | collective-permute-start | bytes 393224 | tf_op jit(solution)/shard_map/ppermute | solution.py:305
  8.3 9.9 %collective-permute-start.1 = (bf16[64,1024]{1,0:T(8,128)(2,1)S(1)}, bf16[64,1024]{1,0:T(8,128)(2,1)S(1)}, u32[]{:S(2)}, u32[]{:S(2)}) collective-permute-start(bf16[64,1024]{1,0:T(8,128)(2,1)S(1)} %get-tuple-element.13.refs_0_.refs_2_), channel_id=1, source_target_pairs={{0,4},{1,5},{2,6},{3,7},{4,8},{5,9},{6,10},{7,11},{8,12},{9,13},{1... | collective-permute-start | bytes 393224 | tf_op jit(solution)/shard_map/ppermute | solution.py:305
  18.2 3.3 %collective-permute-start.3 = (bf16[64,1024]{1,0:T(8,128)(2,1)S(1)}, bf16[64,1024]{1,0:T(8,128)(2,1)S(1)}, u32[]{:S(2)}, u32[]{:S(2)}) collective-permute-start(bf16[64,1024]{1,0:T(8,128)(2,1)S(1)} %broadcast_select_fusion.1), channel_id=1, source_target_pairs={{0,2},{2,0},{4,6},{6,4},{8,10},{10,8},{12,14},{14,12},{16,18},{18,... | collective-permute-start | bytes 393224 | tf_op jit(solution)/shard_map/ppermute | solution.py:309
  18.3 3.2 %collective-permute-start.4 = (bf16[64,1024]{1,0:T(8,128)(2,1)S(1)}, bf16[64,1024]{1,0:T(8,128)(2,1)S(1)}, u32[]{:S(2)}, u32[]{:S(2)}) collective-permute-start(bf16[64,1024]{1,0:T(8,128)(2,1)S(1)} %broadcast_select_fusion), channel_id=1, source_target_pairs={{0,2},{2,0},{4,6},{6,4},{8,10},{10,8},{12,14},{14,12},{16,18},{18,... | collective-permute-start | bytes 393224 | tf_op jit(solution)/shard_map/ppermute | solution.py:309

commit v3 on v2

--- a/solution.py
+++ b/solution.py
@@ -21,10 +21,10 @@
 RUN = 16
 GROUPS = BINS // RUN
 STEP = 16
-BATCH = 8
+BATCH = 4
 SEGMENT = 256
 VMEM_LIMIT = 24 << 20
-MERGED = False
+MERGED = True
 
 F32 = jnp.float32
 BF16 = jnp.bfloat16
@@ -77,32 +77,21 @@
     small[2].wait()
     small[3].wait()
     high_table, low_table = high_ref[...], low_ref[...]
-    reals, imags = [], []
-    live = None
-    for window in range(windows):
-        copy(window).wait()
-        tail_ref[:, :last] = held_ref[window, :, samples - last : samples]
+    def transformed(window):
+        tail_ref[window % 2, :, :last] = held_ref[window, :, samples - last : samples]
         highs, lows = [], []
         for segment in range(segments):
             if segment == segments - 1:
-                piece = tail_ref[...]
+                piece = tail_ref[window % 2]
             else:
                 piece = held_ref[window, :, segment * SEGMENT : (segment + 1) * SEGMENT]
             highs.append(piece.astype(BF16))
             lows.append((piece - highs[-1].astype(F32)).astype(BF16))
         high = jnp.concatenate(highs, axis=0)
         low = jnp.concatenate(lows, axis=0)
-        all_raw = dot(high, high_table) + dot(low, high_table) + dot(high, low_table)
-        if window == 0:
-            for one in (*small[:2], *small[4:]):
-                one.wait()
-            ids = first_ref[0] + lax.broadcasted_iota(jnp.int32, (channels, 1), 0)
-            dead = jnp.where(ids == dead_ref[...], 1.0, 0.0)
-            live = 1.0 - jnp.max(dead, axis=1, keepdims=True)
-            weight_ref[...] = jnp.zeros_like(weight_ref)
-            for offset in range(OFFS):
-                weight = plan_ref[:, offset : offset + 1].astype(F32)
-                weight_ref[offset : offset + 1, :] = jnp.broadcast_to(weight, (1, LANES))
+        return dot(high, high_table) + dot(low, high_table) + dot(high, low_table)
+
+    def whitened(all_raw):
         real = imag = None
         for segment in range(segments):
             raw = all_raw[segment * channels : (segment + 1) * channels]
@@ -116,8 +105,31 @@
         power = real * real + imag * imag
         mean = jnp.sum(power, axis=1, keepdims=True) * (1.0 / BINS)
         factor = lax.rsqrt(power + WATER_LEVEL * mean + EPSILON) * live
-        reals.append(real * factor)
-        imags.append(imag * factor)
+        return real * factor, imag * factor
+
+    pairs = []
+    live = all_raw = None
+    for window in range(windows):
+        if window % 2 == 0:
+            copy(window).wait()
+            copy(window + 1).wait()
+        if window == 1:
+            for one in (*small[:2], *small[4:]):
+                one.wait()
+        now = transformed(window)
+        if window == 1:
+            ids = first_ref[0] + lax.broadcasted_iota(jnp.int32, (channels, 1), 0)
+            dead = jnp.where(ids == dead_ref[...], 1.0, 0.0)
+            live = 1.0 - jnp.max(dead, axis=1, keepdims=True)
+            weight_ref[...] = jnp.zeros_like(weight_ref)
+            for offset in range(OFFS):
+                weight = plan_ref[:, offset : offset + 1].astype(F32)
+                weight_ref[offset : offset + 1, :] = jnp.broadcast_to(weight, (1, LANES))
+        if window > 0:
+            pairs.append(whitened(all_raw))
+        all_raw = now
+    pairs.append(whitened(all_raw))
+    reals, imags = [pair[0] for pair in pairs], [pair[1] for pair in pairs]
     parts = reals + imags
     run_of = lax.broadcasted_iota(jnp.int32, (1, LANES), 1) // RUN
     for bit in (1, 2, 4):
@@ -152,7 +164,7 @@
         out_specs=[vmem] * 3,
         scratch_shapes=[pltpu.VMEM(array.shape, array.dtype) for array in arrays[:-1]]
         + [
-            pltpu.VMEM((channels, SEGMENT), F32),
+            pltpu.VMEM((2, channels, SEGMENT), F32),
             pltpu.SemaphoreType.DMA((windows + len(arrays) - 1,)),
         ],
         compiler_params=pltpu.CompilerParams(vmem_limit_bytes=VMEM_LIMIT),
@@ -249,7 +261,7 @@
             copy(index).start()
         return carry
 
-    lax.fori_loop(0, share // step_rows, one_step, 0)
+    lax.fori_loop(0, share // step_rows, one_step, 0, unroll=True)
     for index in range(share // batch):
         copy(index).wait()
 
@@ -305,6 +317,23 @@
     return lax.ppermute(value, ("chan", "tm"), pairs)
 
 
+def held(value):
+    vmem = pl.BlockSpec(memory_space=pltpu.VMEM)
+
+    def body(in_ref, out_ref):
+        out_ref[...] = in_ref[...]
+
+    return pl.pallas_call(
+        body,
+        out_shape=jax.ShapeDtypeStruct(value.shape, value.dtype),
+        in_specs=[vmem],
+        out_specs=vmem,
+        compiler_params=pltpu.CompilerParams(vmem_limit_bytes=VMEM_LIMIT),
+        cost_estimate=pl.CostEstimate(flops=10**10, bytes_accessed=10**8, transcendentals=0),
+        name="held",
+    )(value)
+
+
 def swapped(value):
     return lax.ppermute(value, "chan", [(block, block ^ 1) for block in range(lax.axis_size("chan"))])
 
@@ -319,6 +348,7 @@
     mine, weights, lags = block_spectra(traces, dead_channels, plan, first_channel, windows * ranks)
     behind = [moved(mine, 2, step) for step in reversed(range(ranks))][::-1]
     own = [mine] + [moved(mine, 0, step) for step in range(1, ranks)]
+    weights = held(weights)
     run = functools.partial(
         correlate, rank=rank, weights=weights, lags=lags, own=own, share=share
     )

time: 24.2 us -> 21.6 us (0.89)
  the two profiles are of different devices: /device:TPU:0 before, /device:TPU:5 now
where the time goes in v3:
time: 21.6 us; the launch traced here: 21.5 us
  waiting for transfers between devices  8.54 us (40%)
  Pallas kernels  8.42 us (39%)
  starting transfers between devices  4.44 us (21%)
    ppermute x3, waiting for transfers between devices, moved(): return lax.ppermute(value, ('chan', 'tm'), pairs)  7.27 us
    pallas_call x2, Pallas kernels, correlate(): pl.pallas_call(functools.partial(correlation_kernel, offsets, sources, sh...  5.3 us
    ppermute x3, starting transfers between devices, moved(): return lax.ppermute(value, ('chan', 'tm'), pairs)  3.71 us
    pallas_call x1, Pallas kernels, block_spectra(): pl.pallas_call(spectra_kernel, out_shape=[jax.ShapeDtypeStruct((channels,...  3.12 us
    ppermute x2, waiting for transfers between devices, swapped(): lax.ppermute(value, 'chan', [(block, block ^ 1) for block in range(lax.ax...  1.27 us
    ppermute x2, starting transfers between devices, swapped(): lax.ppermute(value, 'chan', [(block, block ^ 1) for block in range(lax.ax...  0.73 us
  transfers between devices with their start and end apart: 5, of which 3 were waited for; matrix products, arithmetic and copies ran while one was open for 0% of the time, Pallas kernels for 11%

profile of v3, /device:TPU:5, one launch (start us, length us, event | category | flops | bytes accessed | tf_op | source)
XLA Modules:
  0.0 21.5 jit_solution(13638979191535375338)
XLA Ops:
  0.0 3.1 %spectra.1 = (bf16[64,1024]{1,0:T(8,128)(2,1)S(1)}, f32[8,128]{1,0:T(8,128)S(1)}, bf16[256,129]{1,0:T(8,128)(2,1)S(1)}) custom-call(s32[1]{0:T(128)} %bitcast.1.first_ref, f32[4,64,1500]{2,1,0:T(8,128)} %refs_0_.1, s32[1,96]{1,0:T(1,128)} %bitcast.3, s32[1,3]{1,0:T(1,128)} %refs_2_.1, bf16[256,256]{1,0:T(8,128)(2,1)} %constant.32.clone.refs_3_, ...), custom_call_target="tpu_custom_call" | custom-call | tf_op jit(solution)/shard_map/spectra/pallas_call | solution.py:155
  3.1 2.2 %collective-permute-start.2 = (bf16[64,1024]{1,0:T(8,128)(2,1)S(1)}, bf16[64,1024]{1,0:T(8,128)(2,1)S(1)}, u32[]{:S(2)}, u32[]{:S(2)}) collective-permute-start(bf16[64,1024]{1,0:T(8,128)(2,1)S(1)} %get-tuple-element.13.refs_0_.refs_2_), channel_id=1, source_target_pairs={{0,5},{1,4},{2,7},{3,6},{4,9},{5,8},{6,11},{7,10},{8,13},{9,12},{1... | collective-permute-start | bytes 393224 | tf_op jit(solution)/shard_map/ppermute | solution.py:317
  5.4 1.2 %collective-permute-start.1 = (bf16[64,1024]{1,0:T(8,128)(2,1)S(1)}, bf16[64,1024]{1,0:T(8,128)(2,1)S(1)}, u32[]{:S(2)}, u32[]{:S(2)}) collective-permute-start(bf16[64,1024]{1,0:T(8,128)(2,1)S(1)} %get-tuple-element.13.refs_0_.refs_2_), channel_id=1, source_target_pairs={{0,4},{1,5},{2,6},{3,7},{4,8},{5,9},{6,10},{7,11},{8,12},{9,13},{1... | collective-permute-start | bytes 393224 | tf_op jit(solution)/shard_map/ppermute | solution.py:317
  6.6 0.3 %collective-permute-start = (bf16[64,1024]{1,0:T(8,128)(2,1)S(1)}, bf16[64,1024]{1,0:T(8,128)(2,1)S(1)}, u32[]{:S(2)}, u32[]{:S(2)}) collective-permute-start(bf16[64,1024]{1,0:T(8,128)(2,1)S(1)} %get-tuple-element.13.refs_0_.refs_2_), channel_id=1, source_target_pairs={{0,1},{1,0},{2,3},{3,2},{4,5},{5,4},{6,7},{7,6},{8,9},{9,8},{10,11... | collective-permute-start | bytes 393224 | tf_op jit(solution)/shard_map/ppermute | solution.py:317
  6.8 7.3 %collective-permute-done.refs_1_.refs_3_ = bf16[64,1024]{1,0:T(8,128)(2,1)S(1)} collective-permute-done((bf16[64,1024]{1,0:T(8,128)(2,1)S(1)}, bf16[64,1024]{1,0:T(8,128)(2,1)S(1)}, u32[]{:S(2)}, u32[]{:S(2)}) %collective-permute-start) | collective-permute-done | bytes 131104 | tf_op jit(solution)/shard_map/ppermute | solution.py:317
  14.1 2.3 %correlate_0.1.refs_6_ = f32[1,32,3,64,129]{4,3,2,1,0:T(8,128)} custom-call(s32[1]{0:T(128)} %bitcast.rank_ref, f32[8,128]{1,0:T(8,128)S(1)} %held.1.weight_ref, bf16[256,129]{1,0:T(8,128)(2,1)S(1)} %get-tuple-element.12.lag_ref, bf16[64,1024]{1,0:T(8,128)(2,1)S(1)} %get-tuple-element.13.refs_0_.refs_2_, ...), custom_call_target="tpu_custom_call" | custom-call | flops 268435456 | bytes 2097152 | tf_op jit(solution)/shard_map/correlate_0/pallas_call | solution.py:287
  16.5 0.0 collective-permute-done.2.refs_5_
  16.5 0.0 collective-permute-done.1.refs_4_
  16.5 0.7 %collective-permute-start.4 = (bf16[64,1024]{1,0:T(8,128)(2,1)S(1)}, bf16[64,1024]{1,0:T(8,128)(2,1)S(1)}, u32[]{:S(2)}, u32[]{:S(2)}) collective-permute-start(bf16[64,1024]{1,0:T(8,128)(2,1)S(1)} %broadcast_select_fusion), channel_id=1, source_target_pairs={{0,2},{2,0},{4,6},{6,4},{8,10},{10,8},{12,14},{14,12},{16,18},{18,... | collective-permute-start | bytes 393224 | tf_op jit(solution)/shard_map/ppermute | solution.py:338
  17.2 0.1 collective-permute-start.3
  17.3 0.9 %collective-permute-done.4.refs_3_ = bf16[64,1024]{1,0:T(8,128)(2,1)S(1)} collective-permute-done((bf16[64,1024]{1,0:T(8,128)(2,1)S(1)}, bf16[64,1024]{1,0:T(8,128)(2,1)S(1)}, u32[]{:S(2)}, u32[]{:S(2)}) %collective-permute-start.4) | collective-permute-done | bytes 131104 | tf_op jit(solution)/shard_map/ppermute | solution.py:338
  18.2 0.4 %collective-permute-done.3.refs_2_ = bf16[64,1024]{1,0:T(8,128)(2,1)S(1)} collective-permute-done((bf16[64,1024]{1,0:T(8,128)(2,1)S(1)}, bf16[64,1024]{1,0:T(8,128)(2,1)S(1)}, u32[]{:S(2)}, u32[]{:S(2)}) %collective-permute-start.3) | collective-permute-done | bytes 131104 | tf_op jit(solution)/shard_map/ppermute | solution.py:338
  18.5 3.0 %correlate_1_2.1 = f32[1,32,3,64,129]{4,3,2,1,0:T(8,128)} custom-call(s32[1]{0:T(128)} %bitcast.rank_ref, f32[8,128]{1,0:T(8,128)S(1)} %held.1.weight_ref, bf16[256,129]{1,0:T(8,128)(2,1)S(1)} %get-tuple-element.12.lag_ref, bf16[64,1024]{1,0:T(8,128)(2,1)S(1)} %get-tuple-element.13.refs_0_.refs_2_, ...), custom_call_target="tpu_custom_call", output_to_operand_aliasing={{}: (9, {})} | custom-call | flops 536870912 | bytes 4194304 | tf_op jit(solution)/shard_map/correlate_1_2/pallas_call | solution.py:287
  (3 shorter events, 0.0 us)
Async XLA Ops:
  3.1 13.3 %collective-permute-start.2 = (bf16[64,1024]{1,0:T(8,128)(2,1)S(1)}, bf16[64,1024]{1,0:T(8,128)(2,1)S(1)}, u32[]{:S(2)}, u32[]{:S(2)}) collective-permute-start(bf16[64,1024]{1,0:T(8,128)(2,1)S(1)} %get-tuple-element.13.refs_0_.refs_2_), channel_id=1, source_target_pairs={{0,5},{1,4},{2,7},{3,6},{4,9},{5,8},{6,11},{7,10},{8,13},{9,12},{1... | collective-permute-start | bytes 393224 | tf_op jit(solution)/shard_map/ppermute | solution.py:317
  5.4 11.1 %collective-permute-start.1 = (bf16[64,1024]{1,0:T(8,128)(2,1)S(1)}, bf16[64,1024]{1,0:T(8,128)(2,1)S(1)}, u32[]{:S(2)}, u32[]{:S(2)}) collective-permute-start(bf16[64,1024]{1,0:T(8,128)(2,1)S(1)} %get-tuple-element.13.refs_0_.refs_2_), channel_id=1, source_target_pairs={{0,4},{1,5},{2,6},{3,7},{4,8},{5,9},{6,10},{7,11},{8,12},{9,13},{1... | collective-permute-start | bytes 393224 | tf_op jit(solution)/shard_map/ppermute | solution.py:317
  6.6 7.5 %collective-permute-start = (bf16[64,1024]{1,0:T(8,128)(2,1)S(1)}, bf16[64,1024]{1,0:T(8,128)(2,1)S(1)}, u32[]{:S(2)}, u32[]{:S(2)}) collective-permute-start(bf16[64,1024]{1,0:T(8,128)(2,1)S(1)} %get-tuple-element.13.refs_0_.refs_2_), channel_id=1, source_target_pairs={{0,1},{1,0},{2,3},{3,2},{4,5},{5,4},{6,7},{7,6},{8,9},{9,8},{10,11... | collective-permute-start | bytes 393224 | tf_op jit(solution)/shard_map/ppermute | solution.py:317
  16.5 1.6 %collective-permute-start.4 = (bf16[64,1024]{1,0:T(8,128)(2,1)S(1)}, bf16[64,1024]{1,0:T(8,128)(2,1)S(1)}, u32[]{:S(2)}, u32[]{:S(2)}) collective-permute-start(bf16[64,1024]{1,0:T(8,128)(2,1)S(1)} %broadcast_select_fusion), channel_id=1, source_target_pairs={{0,2},{2,0},{4,6},{6,4},{8,10},{10,8},{12,14},{14,12},{16,18},{18,... | collective-permute-start | bytes 393224 | tf_op jit(solution)/shard_map/ppermute | solution.py:338
  17.2 1.3 %collective-permute-start.3 = (bf16[64,1024]{1,0:T(8,128)(2,1)S(1)}, bf16[64,1024]{1,0:T(8,128)(2,1)S(1)}, u32[]{:S(2)}, u32[]{:S(2)}) collective-permute-start(bf16[64,1024]{1,0:T(8,128)(2,1)S(1)} %broadcast_select_fusion.1), channel_id=1, source_target_pairs={{0,2},{2,0},{4,6},{6,4},{8,10},{10,8},{12,14},{14,12},{16,18},{18,... | collective-permute-start | bytes 393224 | tf_op jit(solution)/shard_map/ppermute | solution.py:338

commit v4 on v3

--- a/solution.py
+++ b/solution.py
@@ -20,11 +20,10 @@
 LANES = 128
 RUN = 16
 GROUPS = BINS // RUN
-STEP = 16
 BATCH = 4
 SEGMENT = 256
 VMEM_LIMIT = 24 << 20
-MERGED = True
+STEPS = (16, 16)
 
 F32 = jnp.float32
 BF16 = jnp.bfloat16
@@ -172,14 +171,37 @@
     )(first_channel, *arrays)
 
 
-def correlation_kernel(offsets, sources, share, step_rows, rank_ref, weight_ref, lag_ref, *refs):
-    own_refs, refs = refs[:sources], refs[sources:]
-    far_refs, refs = refs[: sources * len(offsets)], refs[sources * len(offsets) :]
-    out_ref, near_ref, far_ref, cross_ref, lagged_ref, sems = refs[-6:]
+def row_steps(share):
+    return STEPS if sum(STEPS) == share else (share,)
+
+
+def correlation_kernel(offset, earlier, last, sources, share, rank_ref, weight_ref, lag_ref, *refs):
+    own_refs, far_refs, refs = refs[:sources], refs[sources : 2 * sources], refs[2 * sources :]
+    earlier_ref = out_ref = None
+    if earlier is not None:
+        earlier_ref, refs = refs[0], refs[1:]
+    near_ref, far_ref, cross_ref = refs[-4:-1] if not last else refs[-5:-2]
+    sems = refs[-1]
+    kept_ref = refs[-2] if last else refs[-5]
+    if last:
+        out_ref = refs[-6]
+    elif earlier is not None:
+        out_ref = refs[-6]
     channels = own_refs[0].shape[0]
-    columns = len(offsets) * channels
     pairs = sources // 2
     first_row = rank_ref[0] * share
+    batch = min(BATCH, share)
+    batches = share // batch
+
+    def write_earlier():
+        return pltpu.make_async_copy(earlier_ref, out_ref.at[0, :, earlier], sems.at[batches])
+
+    def write(index):
+        rows = pl.ds(index * batch, batch)
+        return pltpu.make_async_copy(kept_ref.at[rows], out_ref.at[0, rows, offset], sems.at[index])
+
+    if earlier is not None:
+        write_earlier().start()
 
     def lanes_of(source, group):
         start = ((source // 2) * GROUPS + group) * 2 * LANES + (source % 2) * LANES
@@ -196,46 +218,33 @@
                 value = own_ref[:, at]
             near_ref[:, lanes_of(source, group)] = value.astype(F32)
     sign = jnp.where(lax.broadcasted_iota(jnp.int32, (1, LANES), 1) < LANES // 2, -1.0, 1.0)
-    for place, offset in enumerate(offsets):
-        weight = weight_ref[offset : offset + 1, :]
-        turned_weight = weight * sign
-        rows = slice(place * channels, (place + 1) * channels)
-        turned_rows = slice(columns + place * channels, columns + (place + 1) * channels)
-        for source in range(sources):
-            far = far_refs[place * sources + source]
-            lanes = slice((source % 2) * LANES, (source % 2 + 1) * LANES)
-            for group in range(GROUPS):
-                value = far[:, group * LANES : (group + 1) * LANES].astype(F32)
-                turned = pltpu.roll(value, LANES // 2, 1) * turned_weight
-                slot = (source // 2) * GROUPS + group
-                far_ref[slot, rows, lanes] = (value * weight).astype(BF16)
-                far_ref[slot, turned_rows, lanes] = turned.astype(BF16)
+    weight = weight_ref[offset : offset + 1, :]
+    turned_weight = weight * sign
+    for source, far in enumerate(far_refs):
+        lanes = slice((source % 2) * LANES, (source % 2 + 1) * LANES)
+        for group in range(GROUPS):
+            value = far[:, group * LANES : (group + 1) * LANES].astype(F32)
+            turned = pltpu.roll(value, LANES // 2, 1) * turned_weight
+            slot = (source // 2) * GROUPS + group
+            far_ref[slot, :channels, lanes] = (value * weight).astype(BF16)
+            far_ref[slot, channels:, lanes] = turned.astype(BF16)
 
     diagonal = (
         lax.broadcasted_iota(jnp.int32, (RUN, 2 * LANES), 1) % RUN
         == lax.broadcasted_iota(jnp.int32, (RUN, 2 * LANES), 0)
     )
-    column = lax.broadcasted_iota(jnp.int32, (1, 2 * columns), 1) % channels
+    column = lax.broadcasted_iota(jnp.int32, (1, 2 * channels), 1) % channels
     lags = lag_ref[...]
 
-    batch = min(BATCH, step_rows)
-
-    def copy(index):
-        return pltpu.make_async_copy(
-            lagged_ref.at[index],
-            out_ref.at[0, pl.ds(index * batch, batch), pl.ds(offsets[0], len(offsets))],
-            sems.at[index],
-        )
-
-    def one_step(step, carry):
+    def cross_products(first, end):
         for group in range(GROUPS):
             total = None
             for pair in range(pairs):
                 blocks = []
                 slot = pair * GROUPS + group
                 lanes = slice(slot * 2 * LANES, (slot + 1) * 2 * LANES)
-                for row in range(step_rows):
-                    one = near_ref[pl.ds(held_first + step * step_rows + row, 1), lanes]
+                for row in range(first, end):
+                    one = near_ref[pl.ds(held_first + row, 1), lanes]
                     spread = jnp.broadcast_to(one, (RUN, 2 * LANES))
                     blocks.append(jnp.where(diagonal, spread, 0.0).astype(BF16))
                 term = lax.dot_general(
@@ -245,66 +254,84 @@
                     preferred_element_type=F32,
                 )
                 total = term if total is None else total + term
-            for row in range(step_rows):
-                value = total[row * RUN : (row + 1) * RUN]
-                if offsets[0] == 0:
-                    value = jnp.where(column > first_row + step * step_rows + row, value, 0.0)
+            for row in range(first, end):
+                value = total[(row - first) * RUN : (row - first + 1) * RUN]
+                if offset == 0:
+                    value = jnp.where(column > first_row + row, value, 0.0)
                 cross_ref[row, group * RUN : (group + 1) * RUN, :] = value.astype(BF16)
-        for start in range(0, step_rows, batch):
+
+    def lag_sums(first, end):
+        for start in range(first, end, batch):
             sides = []
             for row in range(start, start + batch):
                 cross = cross_ref[row].T
-                sides.append(jnp.concatenate([cross[:columns], cross[columns:]], axis=1))
+                sides.append(jnp.concatenate([cross[:channels], cross[channels:]], axis=1))
             lagged = jnp.dot(jnp.concatenate(sides, axis=0), lags, preferred_element_type=F32)
-            index = (step * step_rows + start) // batch
-            lagged_ref[index] = lagged.reshape(batch, len(offsets), channels, LAGS)
-            copy(index).start()
-        return carry
-
-    lax.fori_loop(0, share // step_rows, one_step, 0, unroll=True)
-    for index in range(share // batch):
-        copy(index).wait()
-
-
-def correlate(offsets, rank, weights, lags, own, far, share, previous=None):
+            kept_ref[start : start + batch] = lagged.reshape(batch, channels, LAGS)
+            if last:
+                write(start // batch).start()
+
+    first = 0
+    for rows in row_steps(share):
+        cross_products(first, first + rows)
+        lag_sums(first, first + rows)
+        first += rows
+    if last:
+        for index in range(batches):
+            write(index).wait()
+    if earlier is not None:
+        write_earlier().wait()
+
+
+def correlate(offset, rank, weights, lags, own, far, share, kept=None, earlier=None, previous=None, last=False):
     sources = len(own)
     channels = own[0].shape[0]
-    count = len(offsets)
     pairs = sources // 2
     vmem = pl.BlockSpec(memory_space=pltpu.VMEM)
-    smem = pl.BlockSpec(memory_space=pltpu.SMEM)
-    hbm = pl.BlockSpec(memory_space=pltpu.HBM)
     arrays = [rank, weights, lags, *own, *far]
-    in_specs = [smem] + [vmem] * (len(arrays) - 1)
-    aliases = {}
+    in_specs = [pl.BlockSpec(memory_space=pltpu.SMEM)] + [vmem] * (len(arrays) - 1)
+    out_shape, out_specs, aliases = [], [], {}
+    if kept is not None:
+        arrays.append(kept)
+        in_specs.append(vmem)
+        out_shape.append(jax.ShapeDtypeStruct((1, share, OFFS, channels, LAGS), F32))
+        out_specs.append(pl.BlockSpec(memory_space=pltpu.HBM))
     if previous is not None:
         aliases = {len(arrays): 0}
         arrays.append(previous)
-        in_specs.append(hbm)
-    step_rows = min(STEP, share)
-    batch = min(BATCH, step_rows)
+        in_specs.append(pl.BlockSpec(memory_space=pltpu.HBM))
+    lagged = (share, channels, LAGS)
+    if not last:
+        out_shape.append(jax.ShapeDtypeStruct(lagged, F32))
+        out_specs.append(vmem)
+    batch = min(BATCH, share)
+    assert all(rows % batch == 0 for rows in row_steps(share))
     held = share if share % 16 == 0 else channels
     return pl.pallas_call(
-        functools.partial(correlation_kernel, offsets, sources, share, step_rows),
-        out_shape=jax.ShapeDtypeStruct((1, share, OFFS, channels, LAGS), F32),
+        functools.partial(correlation_kernel, offset, earlier, last, sources, share),
+        out_shape=out_shape,
         in_specs=in_specs,
-        out_specs=hbm,
+        out_specs=out_specs,
         scratch_shapes=[
             pltpu.VMEM((held, pairs * GROUPS * 2 * LANES), F32),
-            pltpu.VMEM((pairs * GROUPS, 2 * count * channels, 2 * LANES), BF16),
-            pltpu.VMEM((step_rows, BINS, 2 * count * channels), BF16),
-            pltpu.VMEM((share // batch, batch, count, channels, LAGS), F32),
-            pltpu.SemaphoreType.DMA((share // batch,)),
-        ],
+            pltpu.VMEM((pairs * GROUPS, 2 * channels, 2 * LANES), BF16),
+            pltpu.VMEM((share, BINS, 2 * channels), BF16),
+        ]
+        + ([pltpu.VMEM(lagged, F32)] if last else [])
+        + [pltpu.SemaphoreType.DMA((share // batch + 1,))],
         compiler_params=pltpu.CompilerParams(vmem_limit_bytes=VMEM_LIMIT),
         input_output_aliases=aliases,
         cost_estimate=pl.CostEstimate(
-            flops=2 * share * 2 * BINS * 2 * LANES * pairs * channels * count,
-            bytes_accessed=share * count * channels * 2 * LANES * 4,
+            flops=2 * share * 2 * BINS * 2 * LANES * pairs * channels,
+            bytes_accessed=share * channels * 2 * LANES * 4,
             transcendentals=0,
         ),
-        name="correlate_" + "_".join(str(offset) for offset in offsets),
+        name=f"correlate_{offset}",
     )(*arrays)
+
+
+def exchanges(ranks):
+    return [(2, step) for step in range(ranks)] + [(0, step) for step in range(1, ranks)]
 
 
 def moved(value, blocks, ranks):
@@ -317,23 +344,6 @@
     return lax.ppermute(value, ("chan", "tm"), pairs)
 
 
-def held(value):
-    vmem = pl.BlockSpec(memory_space=pltpu.VMEM)
-
-    def body(in_ref, out_ref):
-        out_ref[...] = in_ref[...]
-
-    return pl.pallas_call(
-        body,
-        out_shape=jax.ShapeDtypeStruct(value.shape, value.dtype),
-        in_specs=[vmem],
-        out_specs=vmem,
-        compiler_params=pltpu.CompilerParams(vmem_limit_bytes=VMEM_LIMIT),
-        cost_estimate=pl.CostEstimate(flops=10**10, bytes_accessed=10**8, transcendentals=0),
-        name="held",
-    )(value)
-
-
 def swapped(value):
     return lax.ppermute(value, "chan", [(block, block ^ 1) for block in range(lax.axis_size("chan"))])
 
@@ -342,24 +352,25 @@
     windows, channels, _ = traces.shape
     ranks = lax.axis_size("tm")
     share = channels // ranks
-    assert ranks % 2 == 0 and share % min(STEP, share) == 0
+    assert ranks % 2 == 0
     first_channel = (lax.axis_index("chan") * channels).astype(jnp.int32).reshape(1)
     rank = lax.axis_index("tm").astype(jnp.int32).reshape(1)
     mine, weights, lags = block_spectra(traces, dead_channels, plan, first_channel, windows * ranks)
-    behind = [moved(mine, 2, step) for step in reversed(range(ranks))][::-1]
-    own = [mine] + [moved(mine, 0, step) for step in range(1, ranks)]
-    weights = held(weights)
-    run = functools.partial(
-        correlate, rank=rank, weights=weights, lags=lags, own=own, share=share
-    )
-    result = run((0,), far=own)
-    behind, result = lax.optimization_barrier((behind, result))
+    received = {}
+    for blocks, step in exchanges(ranks):
+        received[blocks, step] = moved(mine, blocks, step)
+    behind = [received[2, step] for step in range(ranks)]
+    own = [mine] + [received[0, step] for step in range(1, ranks)]
     odd = lax.axis_index("chan") % 2 == 1
-    beside = [swapped(jnp.where(odd, far, near)) for far, near in zip(behind, own, strict=True)]
-    if MERGED:
-        return run((1, 2), far=beside + behind, previous=result)
-    result = run((2,), far=behind, previous=result)
-    return run((1,), far=beside, previous=result)
+    run = functools.partial(correlate, rank=rank, weights=weights, lags=lags, own=own, share=share)
+    beside = [swapped(jnp.where(odd, behind[0], mine))]
+    (kept,) = run(0, far=own)
+    later, kept = lax.optimization_barrier((behind[1:], kept))
+    behind = behind[:1] + later
+    beside += [swapped(jnp.where(odd, far, near)) for far, near in zip(behind[1:], own[1:], strict=True)]
+    result, kept = run(2, far=behind, kept=kept, earlier=0)
+    (result,) = run(1, far=beside, kept=kept, earlier=2, previous=result, last=True)
+    return result
 
 
 def solution(mesh):

time: 21.6 us -> 21 us (0.972)
  the two profiles are of different devices: /device:TPU:5 before, /device:TPU:0 now
where the time goes in v4:
time: 21 us; the launch traced here: 20.6 us
  Pallas kernels  8.48 us (40%)
  starting transfers between devices  6.17 us (29%)
  waiting for transfers between devices  5.83 us (28%)
    ppermute x3, starting transfers between devices, moved(): return lax.ppermute(value, ('chan', 'tm'), pairs)  6.03 us
    ppermute x3, waiting for transfers between devices, moved(): return lax.ppermute(value, ('chan', 'tm'), pairs)  5.82 us
    pallas_call x3, Pallas kernels, correlate(): pl.pallas_call(functools.partial(correlation_kernel, offset, earlier, las...  5.35 us
    pallas_call x1, Pallas kernels, block_spectra(): pl.pallas_call(spectra_kernel, out_shape=[jax.ShapeDtypeStruct((channels,...  3.12 us
  transfers between devices with their start and end apart: 5, of which 3 were waited for; matrix products, arithmetic and copies ran while one was open for 0% of the time, Pallas kernels for 15%

profile of v4, /device:TPU:0, one launch (start us, length us, event | category | flops | bytes accessed | tf_op | source)
XLA Modules:
  0.0 20.6 jit_solution(9574754229749424193)
XLA Ops:
  0.0 3.1 %spectra.1 = (bf16[64,1024]{1,0:T(8,128)(2,1)S(1)}, f32[8,128]{1,0:T(8,128)S(1)}, bf16[256,129]{1,0:T(8,128)(2,1)S(1)}) custom-call(s32[1]{0:T(128)} %bitcast.1.first_ref, f32[4,64,1500]{2,1,0:T(8,128)} %refs_0_.1, s32[1,96]{1,0:T(1,128)} %bitcast.3, s32[1,3]{1,0:T(1,128)} %refs_2_.1, bf16[256,256]{1,0:T(8,128)(2,1)} %constant.32.clone.refs_3_, ...), custom_call_target="tpu_custom_call" | custom-call | tf_op jit(solution)/shard_map/spectra/pallas_call | solution.py:154
  3.1 3.0 %collective-permute-start.1 = (bf16[64,1024]{1,0:T(8,128)(2,1)S(1)}, bf16[64,1024]{1,0:T(8,128)(2,1)S(1)}, u32[]{:S(2)}, u32[]{:S(2)}) collective-permute-start(bf16[64,1024]{1,0:T(8,128)(2,1)S(1)} %get-tuple-element.14.refs_0_.refs_2_), channel_id=1, source_target_pairs={{0,4},{1,5},{2,6},{3,7},{4,8},{5,9},{6,10},{7,11},{8,12},{9,13},{1... | collective-permute-start | bytes 393224 | tf_op jit(solution)/shard_map/ppermute | solution.py:344
  6.2 2.4 %collective-permute-start.3 = (bf16[64,1024]{1,0:T(8,128)(2,1)S(1)}, bf16[64,1024]{1,0:T(8,128)(2,1)S(1)}, u32[]{:S(2)}, u32[]{:S(2)}) collective-permute-start(bf16[64,1024]{1,0:T(8,128)(2,1)S(1)} %get-tuple-element.14.refs_0_.refs_2_), channel_id=1, source_target_pairs={{0,5},{1,4},{2,7},{3,6},{4,9},{5,8},{6,11},{7,10},{8,13},{9,12},{1... | collective-permute-start | bytes 393224 | tf_op jit(solution)/shard_map/ppermute | solution.py:344
  8.6 0.5 %collective-permute-start = (bf16[64,1024]{1,0:T(8,128)(2,1)S(1)}, bf16[64,1024]{1,0:T(8,128)(2,1)S(1)}, u32[]{:S(2)}, u32[]{:S(2)}) collective-permute-start(bf16[64,1024]{1,0:T(8,128)(2,1)S(1)} %get-tuple-element.14.refs_0_.refs_2_), channel_id=1, source_target_pairs={{0,1},{1,0},{2,3},{3,2},{4,5},{5,4},{6,7},{7,6},{8,9},{9,8},{10,11... | collective-permute-start | bytes 393224 | tf_op jit(solution)/shard_map/ppermute | solution.py:344
  9.2 4.3 %collective-permute-done.1.refs_2_ = bf16[64,1024]{1,0:T(8,128)(2,1)S(1)} collective-permute-done((bf16[64,1024]{1,0:T(8,128)(2,1)S(1)}, bf16[64,1024]{1,0:T(8,128)(2,1)S(1)}, u32[]{:S(2)}, u32[]{:S(2)}) %collective-permute-start.1) | collective-permute-done | bytes 131104 | tf_op jit(solution)/shard_map/ppermute | solution.py:344
  13.5 0.1 collective-permute-start.2
  13.6 1.4 %collective-permute-done.refs_1_.refs_3_ = bf16[64,1024]{1,0:T(8,128)(2,1)S(1)} collective-permute-done((bf16[64,1024]{1,0:T(8,128)(2,1)S(1)}, bf16[64,1024]{1,0:T(8,128)(2,1)S(1)}, u32[]{:S(2)}, u32[]{:S(2)}) %collective-permute-start) | collective-permute-done | bytes 131104 | tf_op jit(solution)/shard_map/ppermute | solution.py:344
  14.9 1.5 %correlate_0.1.refs_4_ = f32[32,64,129]{2,1,0:T(8,128)S(1)} custom-call(s32[1]{0:T(128)} %bitcast.rank_ref, f32[8,128]{1,0:T(8,128)S(1)} %get-tuple-element.12.weight_ref, bf16[256,129]{1,0:T(8,128)(2,1)S(1)} %get-tuple-element.13.lag_ref, bf16[64,1024]{1,0:T(8,128)(2,1)S(1)} %get-tuple-element.14.refs_0_.refs_2_, ...), custom_call_target="tpu_custom_call" | custom-call | flops 268435456 | bytes 2097152 | tf_op jit(solution)/shard_map/correlate_0/pallas_call | solution.py:310
  16.4 0.1 collective-permute-done.3.refs_3_
  16.6 0.1 collective-permute-start.4
  16.6 1.6 %correlate_2.1 = (f32[1,32,3,64,129]{4,3,2,1,0:T(8,128)}, f32[32,64,129]{2,1,0:T(8,128)S(1)}) custom-call(s32[1]{0:T(128)} %bitcast.rank_ref, f32[8,128]{1,0:T(8,128)S(1)} %get-tuple-element.12.weight_ref, bf16[256,129]{1,0:T(8,128)(2,1)S(1)} %get-tuple-element.13.lag_ref, bf16[64,1024]{1,0:T(8,128)(2,1)S(1)} %get-tuple-element.14.refs_0_.refs_2_, ...), custom_call_target="tpu_custom_call" | custom-call | flops 268435456 | bytes 2097152 | tf_op jit(solution)/shard_map/correlate_2/pallas_call | solution.py:310
  18.2 0.0 collective-permute-done.2.refs_2_
  18.2 0.0 collective-permute-done.4.refs_3_
  18.2 2.3 %correlate_1.1 = f32[1,32,3,64,129]{4,3,2,1,0:T(8,128)} custom-call(s32[1]{0:T(128)} %bitcast.rank_ref, f32[8,128]{1,0:T(8,128)S(1)} %get-tuple-element.12.weight_ref, bf16[256,129]{1,0:T(8,128)(2,1)S(1)} %get-tuple-element.13.lag_ref, bf16[64,1024]{1,0:T(8,128)(2,1)S(1)} %get-tuple-element.14.refs_0_.refs_2_, ...), custom_call_target="tpu_custom_call", output_to_operand_aliasing={{}: (8, {})} | custom-call | flops 268435456 | bytes 2097152 | tf_op jit(solution)/shard_map/correlate_1/pallas_call | solution.py:310
  (2 shorter events, 0.0 us)
Async XLA Ops:
  3.1 10.3 %collective-permute-start.1 = (bf16[64,1024]{1,0:T(8,128)(2,1)S(1)}, bf16[64,1024]{1,0:T(8,128)(2,1)S(1)}, u32[]{:S(2)}, u32[]{:S(2)}) collective-permute-start(bf16[64,1024]{1,0:T(8,128)(2,1)S(1)} %get-tuple-element.14.refs_0_.refs_2_), channel_id=1, source_target_pairs={{0,4},{1,5},{2,6},{3,7},{4,8},{5,9},{6,10},{7,11},{8,12},{9,13},{1... | collective-permute-start | bytes 393224 | tf_op jit(solution)/shard_map/ppermute | solution.py:344
  6.2 10.4 %collective-permute-start.3 = (bf16[64,1024]{1,0:T(8,128)(2,1)S(1)}, bf16[64,1024]{1,0:T(8,128)(2,1)S(1)}, u32[]{:S(2)}, u32[]{:S(2)}) collective-permute-start(bf16[64,1024]{1,0:T(8,128)(2,1)S(1)} %get-tuple-element.14.refs_0_.refs_2_), channel_id=1, source_target_pairs={{0,5},{1,4},{2,7},{3,6},{4,9},{5,8},{6,11},{7,10},{8,13},{9,12},{1... | collective-permute-start | bytes 393224 | tf_op jit(solution)/shard_map/ppermute | solution.py:344
  8.6 6.3 %collective-permute-start = (bf16[64,1024]{1,0:T(8,128)(2,1)S(1)}, bf16[64,1024]{1,0:T(8,128)(2,1)S(1)}, u32[]{:S(2)}, u32[]{:S(2)}) collective-permute-start(bf16[64,1024]{1,0:T(8,128)(2,1)S(1)} %get-tuple-element.14.refs_0_.refs_2_), channel_id=1, source_target_pairs={{0,1},{1,0},{2,3},{3,2},{4,5},{5,4},{6,7},{7,6},{8,9},{9,8},{10,11... | collective-permute-start | bytes 393224 | tf_op jit(solution)/shard_map/ppermute | solution.py:344
  13.5 4.7 %collective-permute-start.2 = (bf16[64,1024]{1,0:T(8,128)(2,1)S(1)}, bf16[64,1024]{1,0:T(8,128)(2,1)S(1)}, u32[]{:S(2)}, u32[]{:S(2)}) collective-permute-start(bf16[64,1024]{1,0:T(8,128)(2,1)S(1)} %broadcast_select_fusion.1), channel_id=1, source_target_pairs={{0,2},{2,0},{4,6},{6,4},{8,10},{10,8},{12,14},{14,12},{16,18},{18,... | collective-permute-start | bytes 393224 | tf_op jit(solution)/shard_map/ppermute | solution.py:348
  16.6 1.6 %collective-permute-start.4 = (bf16[64,1024]{1,0:T(8,128)(2,1)S(1)}, bf16[64,1024]{1,0:T(8,128)(2,1)S(1)}, u32[]{:S(2)}, u32[]{:S(2)}) collective-permute-start(bf16[64,1024]{1,0:T(8,128)(2,1)S(1)} %broadcast_select_fusion), channel_id=1, source_target_pairs={{0,2},{2,0},{4,6},{6,4},{8,10},{10,8},{12,14},{14,12},{16,18},{18,... | collective-permute-start | bytes 393224 | tf_op jit(solution)/shard_map/ppermute | solution.py:348

commit v5 on v4

--- a/solution.py
+++ b/solution.py
@@ -76,24 +76,26 @@
     small[2].wait()
     small[3].wait()
     high_table, low_table = high_ref[...], low_ref[...]
-    def transformed(window):
-        tail_ref[window % 2, :, :last] = held_ref[window, :, samples - last : samples]
+    def transformed():
         highs, lows = [], []
         for segment in range(segments):
-            if segment == segments - 1:
-                piece = tail_ref[window % 2]
-            else:
-                piece = held_ref[window, :, segment * SEGMENT : (segment + 1) * SEGMENT]
-            highs.append(piece.astype(BF16))
-            lows.append((piece - highs[-1].astype(F32)).astype(BF16))
+            for window in range(windows):
+                if segment == segments - 1:
+                    tail_ref[window, :, :last] = held_ref[window, :, samples - last : samples]
+                    piece = tail_ref[window]
+                else:
+                    piece = held_ref[window, :, segment * SEGMENT : (segment + 1) * SEGMENT]
+                highs.append(piece.astype(BF16))
+                lows.append((piece - highs[-1].astype(F32)).astype(BF16))
         high = jnp.concatenate(highs, axis=0)
         low = jnp.concatenate(lows, axis=0)
         return dot(high, high_table) + dot(low, high_table) + dot(high, low_table)
 
-    def whitened(all_raw):
+    def whitened(all_raw, window):
         real = imag = None
         for segment in range(segments):
-            raw = all_raw[segment * channels : (segment + 1) * channels]
+            start = (segment * windows + window) * channels
+            raw = all_raw[start : start + channels]
             if segment == 0:
                 real, imag = raw[:, :BINS], raw[:, BINS:]
             else:
@@ -106,32 +108,23 @@
         factor = lax.rsqrt(power + WATER_LEVEL * mean + EPSILON) * live
         return real * factor, imag * factor
 
-    pairs = []
-    live = all_raw = None
     for window in range(windows):
-        if window % 2 == 0:
-            copy(window).wait()
-            copy(window + 1).wait()
-        if window == 1:
-            for one in (*small[:2], *small[4:]):
-                one.wait()
-        now = transformed(window)
-        if window == 1:
-            ids = first_ref[0] + lax.broadcasted_iota(jnp.int32, (channels, 1), 0)
-            dead = jnp.where(ids == dead_ref[...], 1.0, 0.0)
-            live = 1.0 - jnp.max(dead, axis=1, keepdims=True)
-            weight_ref[...] = jnp.zeros_like(weight_ref)
-            for offset in range(OFFS):
-                weight = plan_ref[:, offset : offset + 1].astype(F32)
-                weight_ref[offset : offset + 1, :] = jnp.broadcast_to(weight, (1, LANES))
-        if window > 0:
-            pairs.append(whitened(all_raw))
-        all_raw = now
-    pairs.append(whitened(all_raw))
+        copy(window).wait()
+    for one in (*small[:2], *small[4:]):
+        one.wait()
+    all_raw = transformed()
+    ids = first_ref[0] + lax.broadcasted_iota(jnp.int32, (channels, 1), 0)
+    dead = jnp.where(ids == dead_ref[...], 1.0, 0.0)
+    live = 1.0 - jnp.max(dead, axis=1, keepdims=True)
+    weight_ref[...] = jnp.zeros_like(weight_ref)
+    for offset in range(OFFS):
+        weight = plan_ref[:, offset : offset + 1].astype(F32)
+        weight_ref[offset : offset + 1, :] = jnp.broadcast_to(weight, (1, LANES))
+    pairs = [whitened(all_raw, window) for window in range(windows)]
     reals, imags = [pair[0] for pair in pairs], [pair[1] for pair in pairs]
     parts = reals + imags
     run_of = lax.broadcasted_iota(jnp.int32, (1, LANES), 1) // RUN
-    for bit in (1, 2, 4):
+    for bit in (4, 1, 2):
         keep = (run_of & bit) == 0
         for index in range(len(parts)):
             if index & bit:
@@ -163,7 +156,7 @@
         out_specs=[vmem] * 3,
         scratch_shapes=[pltpu.VMEM(array.shape, array.dtype) for array in arrays[:-1]]
         + [
-            pltpu.VMEM((2, channels, SEGMENT), F32),
+            pltpu.VMEM((windows, channels, SEGMENT), F32),
             pltpu.SemaphoreType.DMA((windows + len(arrays) - 1,)),
         ],
         compiler_params=pltpu.CompilerParams(vmem_limit_bytes=VMEM_LIMIT),

time: 21 us -> 20.6 us (0.981)
  Pallas kernels: 8.48 us -> 8.13 us
    pallas_call x1, Pallas kernels: 3.12 us -> 2.77 us  [block_spectra(): pl.pallas_call(spectra_kernel, out_shape=[jax.ShapeDtypeStruct((channels,...]
where the time goes in v5:
time: 20.6 us; the launch traced here: 20.2 us
  Pallas kernels  8.13 us (39%)
  starting transfers between devices  6.17 us (30%)
  waiting for transfers between devices  5.82 us (28%)
    ppermute x3, starting transfers between devices, moved(): return lax.ppermute(value, ('chan', 'tm'), pairs)  6.02 us
    ppermute x3, waiting for transfers between devices, moved(): return lax.ppermute(value, ('chan', 'tm'), pairs)  5.81 us
    pallas_call x3, Pallas kernels, correlate(): pl.pallas_call(functools.partial(correlation_kernel, offset, earlier, las...  5.36 us
    pallas_call x1, Pallas kernels, block_spectra(): pl.pallas_call(spectra_kernel, out_shape=[jax.ShapeDtypeStruct((channels,...  2.77 us
  transfers between devices with their start and end apart: 5, of which 3 were waited for; matrix products, arithmetic and copies ran while one was open for 0% of the time, Pallas kernels for 15%

profile of v5, /device:TPU:0, one launch (start us, length us, event | category | flops | bytes accessed | tf_op | source)
XLA Modules:
  0.0 20.2 jit_solution(11239848429042942639)
XLA Ops:
  0.0 2.8 %spectra.1 = (bf16[64,1024]{1,0:T(8,128)(2,1)S(1)}, f32[8,128]{1,0:T(8,128)S(1)}, bf16[256,129]{1,0:T(8,128)(2,1)S(1)}) custom-call(s32[1]{0:T(128)} %bitcast.1.first_ref, f32[4,64,1500]{2,1,0:T(8,128)} %refs_0_.1, s32[1,96]{1,0:T(1,128)} %bitcast.3, s32[1,3]{1,0:T(1,128)} %refs_2_.1, bf16[256,256]{1,0:T(8,128)(2,1)} %constant.32.clone.refs_3_, ...), custom_call_target="tpu_custom_call" | custom-call | tf_op jit(solution)/shard_map/spectra/pallas_call | solution.py:147
  2.8 3.0 %collective-permute-start.1 = (bf16[64,1024]{1,0:T(8,128)(2,1)S(1)}, bf16[64,1024]{1,0:T(8,128)(2,1)S(1)}, u32[]{:S(2)}, u32[]{:S(2)}) collective-permute-start(bf16[64,1024]{1,0:T(8,128)(2,1)S(1)} %get-tuple-element.14.refs_0_.refs_2_), channel_id=1, source_target_pairs={{0,4},{1,5},{2,6},{3,7},{4,8},{5,9},{6,10},{7,11},{8,12},{9,13},{1... | collective-permute-start | bytes 393224 | tf_op jit(solution)/shard_map/ppermute | solution.py:337
  5.8 2.4 %collective-permute-start.3 = (bf16[64,1024]{1,0:T(8,128)(2,1)S(1)}, bf16[64,1024]{1,0:T(8,128)(2,1)S(1)}, u32[]{:S(2)}, u32[]{:S(2)}) collective-permute-start(bf16[64,1024]{1,0:T(8,128)(2,1)S(1)} %get-tuple-element.14.refs_0_.refs_2_), channel_id=1, source_target_pairs={{0,5},{1,4},{2,7},{3,6},{4,9},{5,8},{6,11},{7,10},{8,13},{9,12},{1... | collective-permute-start | bytes 393224 | tf_op jit(solution)/shard_map/ppermute | solution.py:337
  8.3 0.5 %collective-permute-start = (bf16[64,1024]{1,0:T(8,128)(2,1)S(1)}, bf16[64,1024]{1,0:T(8,128)(2,1)S(1)}, u32[]{:S(2)}, u32[]{:S(2)}) collective-permute-start(bf16[64,1024]{1,0:T(8,128)(2,1)S(1)} %get-tuple-element.14.refs_0_.refs_2_), channel_id=1, source_target_pairs={{0,1},{1,0},{2,3},{3,2},{4,5},{5,4},{6,7},{7,6},{8,9},{9,8},{10,11... | collective-permute-start | bytes 393224 | tf_op jit(solution)/shard_map/ppermute | solution.py:337
  8.8 4.3 %collective-permute-done.1.refs_2_ = bf16[64,1024]{1,0:T(8,128)(2,1)S(1)} collective-permute-done((bf16[64,1024]{1,0:T(8,128)(2,1)S(1)}, bf16[64,1024]{1,0:T(8,128)(2,1)S(1)}, u32[]{:S(2)}, u32[]{:S(2)}) %collective-permute-start.1) | collective-permute-done | bytes 131104 | tf_op jit(solution)/shard_map/ppermute | solution.py:337
  13.1 0.1 collective-permute-start.2
  13.2 1.4 %collective-permute-done.refs_1_.refs_3_ = bf16[64,1024]{1,0:T(8,128)(2,1)S(1)} collective-permute-done((bf16[64,1024]{1,0:T(8,128)(2,1)S(1)}, bf16[64,1024]{1,0:T(8,128)(2,1)S(1)}, u32[]{:S(2)}, u32[]{:S(2)}) %collective-permute-start) | collective-permute-done | bytes 131104 | tf_op jit(solution)/shard_map/ppermute | solution.py:337
  14.6 1.5 %correlate_0.1.refs_4_ = f32[32,64,129]{2,1,0:T(8,128)S(1)} custom-call(s32[1]{0:T(128)} %bitcast.rank_ref, f32[8,128]{1,0:T(8,128)S(1)} %get-tuple-element.12.weight_ref, bf16[256,129]{1,0:T(8,128)(2,1)S(1)} %get-tuple-element.13.lag_ref, bf16[64,1024]{1,0:T(8,128)(2,1)S(1)} %get-tuple-element.14.refs_0_.refs_2_, ...), custom_call_target="tpu_custom_call" | custom-call | flops 268435456 | bytes 2097152 | tf_op jit(solution)/shard_map/correlate_0/pallas_call | solution.py:303
  16.1 0.1 collective-permute-done.3.refs_3_
  16.2 0.1 collective-permute-start.4
  16.3 1.6 %correlate_2.1 = (f32[1,32,3,64,129]{4,3,2,1,0:T(8,128)}, f32[32,64,129]{2,1,0:T(8,128)S(1)}) custom-call(s32[1]{0:T(128)} %bitcast.rank_ref, f32[8,128]{1,0:T(8,128)S(1)} %get-tuple-element.12.weight_ref, bf16[256,129]{1,0:T(8,128)(2,1)S(1)} %get-tuple-element.13.lag_ref, bf16[64,1024]{1,0:T(8,128)(2,1)S(1)} %get-tuple-element.14.refs_0_.refs_2_, ...), custom_call_target="tpu_custom_call" | custom-call | flops 268435456 | bytes 2097152 | tf_op jit(solution)/shard_map/correlate_2/pallas_call | solution.py:303
  17.9 0.0 collective-permute-done.2.refs_2_
  17.9 0.0 collective-permute-done.4.refs_3_
  17.9 2.3 %correlate_1.1 = f32[1,32,3,64,129]{4,3,2,1,0:T(8,128)} custom-call(s32[1]{0:T(128)} %bitcast.rank_ref, f32[8,128]{1,0:T(8,128)S(1)} %get-tuple-element.12.weight_ref, bf16[256,129]{1,0:T(8,128)(2,1)S(1)} %get-tuple-element.13.lag_ref, bf16[64,1024]{1,0:T(8,128)(2,1)S(1)} %get-tuple-element.14.refs_0_.refs_2_, ...), custom_call_target="tpu_custom_call", output_to_operand_aliasing={{}: (8, {})} | custom-call | flops 268435456 | bytes 2097152 | tf_op jit(solution)/shard_map/correlate_1/pallas_call | solution.py:303
  (2 shorter events, 0.0 us)
Async XLA Ops:
  2.8 10.3 %collective-permute-start.1 = (bf16[64,1024]{1,0:T(8,128)(2,1)S(1)}, bf16[64,1024]{1,0:T(8,128)(2,1)S(1)}, u32[]{:S(2)}, u32[]{:S(2)}) collective-permute-start(bf16[64,1024]{1,0:T(8,128)(2,1)S(1)} %get-tuple-element.14.refs_0_.refs_2_), channel_id=1, source_target_pairs={{0,4},{1,5},{2,6},{3,7},{4,8},{5,9},{6,10},{7,11},{8,12},{9,13},{1... | collective-permute-start | bytes 393224 | tf_op jit(solution)/shard_map/ppermute | solution.py:337
  5.8 10.4 %collective-permute-start.3 = (bf16[64,1024]{1,0:T(8,128)(2,1)S(1)}, bf16[64,1024]{1,0:T(8,128)(2,1)S(1)}, u32[]{:S(2)}, u32[]{:S(2)}) collective-permute-start(bf16[64,1024]{1,0:T(8,128)(2,1)S(1)} %get-tuple-element.14.refs_0_.refs_2_), channel_id=1, source_target_pairs={{0,5},{1,4},{2,7},{3,6},{4,9},{5,8},{6,11},{7,10},{8,13},{9,12},{1... | collective-permute-start | bytes 393224 | tf_op jit(solution)/shard_map/ppermute | solution.py:337
  8.3 6.3 %collective-permute-start = (bf16[64,1024]{1,0:T(8,128)(2,1)S(1)}, bf16[64,1024]{1,0:T(8,128)(2,1)S(1)}, u32[]{:S(2)}, u32[]{:S(2)}) collective-permute-start(bf16[64,1024]{1,0:T(8,128)(2,1)S(1)} %get-tuple-element.14.refs_0_.refs_2_), channel_id=1, source_target_pairs={{0,1},{1,0},{2,3},{3,2},{4,5},{5,4},{6,7},{7,6},{8,9},{9,8},{10,11... | collective-permute-start | bytes 393224 | tf_op jit(solution)/shard_map/ppermute | solution.py:337
  13.1 4.7 %collective-permute-start.2 = (bf16[64,1024]{1,0:T(8,128)(2,1)S(1)}, bf16[64,1024]{1,0:T(8,128)(2,1)S(1)}, u32[]{:S(2)}, u32[]{:S(2)}) collective-permute-start(bf16[64,1024]{1,0:T(8,128)(2,1)S(1)} %broadcast_select_fusion.1), channel_id=1, source_target_pairs={{0,2},{2,0},{4,6},{6,4},{8,10},{10,8},{12,14},{14,12},{16,18},{18,... | collective-permute-start | bytes 393224 | tf_op jit(solution)/shard_map/ppermute | solution.py:341
  16.2 1.7 %collective-permute-start.4 = (bf16[64,1024]{1,0:T(8,128)(2,1)S(1)}, bf16[64,1024]{1,0:T(8,128)(2,1)S(1)}, u32[]{:S(2)}, u32[]{:S(2)}) collective-permute-start(bf16[64,1024]{1,0:T(8,128)(2,1)S(1)} %broadcast_select_fusion), channel_id=1, source_target_pairs={{0,2},{2,0},{4,6},{6,4},{8,10},{10,8},{12,14},{14,12},{16,18},{18,... | collective-permute-start | bytes 393224 | tf_op jit(solution)/shard_map/ppermute | solution.py:341
